TPU v7x, 32 devices: a whole 2x2x4 slice. The times are simulated.
32 devices in a mesh: row: 8 (over y, x, core), col: 4 (over z).
Axes of the slice: x: 2, y: 2, z: 4, core: 2. Of those that a mesh axis runs over, the one named last changes fastest.
Arguments:
- hessenberg: float32 [16384, 16384], P('row', 'col'), may hold values from -6 to 6, as said below
- factors: float32 [3, 32, 512, 512], P(None, 'row', 'col'), may hold values from -1 to 1, as said below
- active: int32 [3, 32], replicated, may hold values 0 or 1
Outputs:
- updated_slab: float32 [16384, 16384], P('row', 'col')
Inputs may be any that keep to these rules, and one draw needn't show every extreme that they name: `hessenberg`: in global order, zero below the first subdiagonal. Each factors[f, s] is orthogonal up to float32 rounding.
All inputs are finite; a program needn't handle non-finite values.
Results may differ from a plain program's by a relative error of at most 0.0001.
Values sent between devices are 32-bit elements; how exact they have to be, the bound alone decides.
No kernel may reach another device: no remote copies, remote signals or barrier semaphores. Data moves between devices by JAX's collectives and lax.ppermute only.
A program may use at most 256 MiB of HBM per device.

v0:
```python
import jax
import jax.numpy as jnp
from jax import lax
from jax.sharding import PartitionSpec as P

PRECISE = lax.Precision.HIGHEST


def passed_along(value, axis, steps):
    count = lax.axis_size(axis)
    pairs = [(source, (source + steps) % count) for source in range(count)]
    return lax.ppermute(value, axis, pairs)


def left_apply(factor, stacked):
    return jnp.einsum("kab,kan->kbn", factor, stacked, precision=PRECISE)


def right_apply(stacked, factor):
    return jnp.einsum("nka,kab->nkb", stacked, factor, precision=PRECISE)


def effective(factor, flag_row):
    identity = jnp.eye(factor.shape[-1], dtype=jnp.float32)
    return jnp.where(flag_row[:, None, None] > 0, factor, identity)


def wrap_fix(received, at_edge, offset_by, along_dim):
    return jnp.where(at_edge, jnp.roll(received, offset_by, axis=along_dim), received)


def sort_columns(collected, grid_rows, grid_cols, col_blocks):
    phases, all_blocks, pieces, window = collected.shape
    natural = collected.reshape(
        phases, grid_rows, all_blocks // grid_rows, pieces, window
    ).transpose(0, 2, 1, 3, 4)
    return natural.reshape(phases, col_blocks, grid_cols, pieces, window).transpose(0, 2, 1, 3, 4)


def local(hessenberg, factors, active):
    rows_here, cols_here = hessenberg.shape
    window = factors.shape[-1]
    half_win = window // 2
    phases = factors.shape[0]
    grid_rows = lax.axis_size("row")
    grid_cols = lax.axis_size("col")
    row_index = lax.axis_index("row")
    col_index = lax.axis_index("col")
    row_blocks = rows_here // window
    col_blocks = cols_here // window
    all_blocks = row_blocks * grid_rows
    slot_row = jnp.arange(row_blocks, dtype=jnp.int32) * grid_rows + row_index
    slot_col = jnp.arange(col_blocks, dtype=jnp.int32) * grid_cols + col_index
    within = jnp.arange(window, dtype=jnp.int32)
    glob_row = (slot_row[:, None] * window + within[None, :]).reshape(rows_here)
    glob_col = (slot_col[:, None] * window + within[None, :]).reshape(cols_here)
    current = hessenberg
    for phase_idx in range(phases):
        chosen = factors[phase_idx : phase_idx + 1]
        row_raw = lax.all_gather(chosen, "col", axis=2, tiled=True)[0]
        gathered = lax.all_gather(chosen, "row", axis=1, tiled=True)
        col_raw = lax.all_to_all(
            sort_columns(gathered, grid_rows, grid_cols, col_blocks),
            "col",
            split_axis=1,
            concat_axis=3,
            tiled=True,
        )
        col_raw = col_raw.reshape(col_blocks, window, window)
        flag_all = active[phase_idx]
        row_flag = jnp.take(flag_all, slot_row)
        col_flag = jnp.take(flag_all, slot_col)
        if phase_idx % 2 == 1:
            row_flag = jnp.where(slot_row < all_blocks - 1, row_flag, 0)
            col_flag = jnp.where(slot_col < all_blocks - 1, col_flag, 0)
        row_factor = effective(row_raw, row_flag)
        col_factor = effective(col_raw, col_flag)
        blocks = current.reshape(row_blocks, window, cols_here)
        if phase_idx % 2 == 0:
            updated = left_apply(row_factor, blocks)
            keep_mask = glob_col[None, :] >= (slot_row[:, None] + 1) * window
            current = jnp.where(keep_mask[:, None, :], updated, blocks).reshape(
                rows_here, cols_here
            )
            columns = current.reshape(rows_here, col_blocks, window)
            updated = right_apply(columns, col_factor)
            keep_mask = glob_row[:, None] < slot_col[None, :] * window
            current = jnp.where(keep_mask[:, :, None], updated, columns).reshape(
                rows_here, cols_here
            )
        else:
            top_half = blocks[:, :half_win]
            bottoms = blocks[:, half_win:]
            from_below = wrap_fix(
                passed_along(top_half, "row", -1), row_index == grid_rows - 1, -1, 0
            )
            from_above = wrap_fix(passed_along(bottoms, "row", 1), row_index == 0, 1, 0)
            prior_factor = wrap_fix(
                passed_along(row_factor[:, :, half_win:], "row", 1), row_index == 0, 1, 0
            )
            new_bottom = left_apply(
                row_factor[:, :, :half_win], jnp.concatenate([bottoms, from_below], axis=1)
            )
            keep_mask = glob_col[None, :] >= slot_row[:, None] * window + window + half_win
            new_bottom = jnp.where(keep_mask[:, None, :], new_bottom, bottoms)
            new_top = left_apply(prior_factor, jnp.concatenate([from_above, top_half], axis=1))
            keep_mask = glob_col[None, :] >= slot_row[:, None] * window + half_win
            new_top = jnp.where(keep_mask[:, None, :], new_top, top_half)
            current = jnp.concatenate([new_top, new_bottom], axis=1).reshape(rows_here, cols_here)
            columns = current.reshape(rows_here, col_blocks, window)
            left_half = columns[:, :, :half_win]
            right_half = columns[:, :, half_win:]
            from_right = wrap_fix(
                passed_along(left_half, "col", -1), col_index == grid_cols - 1, -1, 1
            )
            from_left = wrap_fix(passed_along(right_half, "col", 1), col_index == 0, 1, 1)
            prior_factor = wrap_fix(
                passed_along(col_factor[:, :, half_win:], "col", 1), col_index == 0, 1, 0
            )
            new_right = right_apply(
                jnp.concatenate([right_half, from_right], axis=2), col_factor[:, :, :half_win]
            )
            keep_mask = glob_row[:, None] < slot_col[None, :] * window + half_win
            new_right = jnp.where(keep_mask[:, :, None], new_right, right_half)
            new_left = right_apply(jnp.concatenate([from_left, left_half], axis=2), prior_factor)
            keep_mask = glob_row[:, None] < slot_col[None, :] * window - half_win
            new_left = jnp.where(keep_mask[:, :, None], new_left, left_half)
            current = jnp.concatenate([new_left, new_right], axis=2).reshape(rows_here, cols_here)
    return current


def solution(mesh):
    return jax.shard_map(
        local,
        mesh=mesh,
        in_specs=(P("row", "col"), P(None, "row", "col", None), P()),
        out_specs=P("row", "col"),
        check_vma=False,
    )
```

profile of v0, /device:TPU:20, one launch (start us, length us, event | category | flops | bytes accessed | tf_op | source)
XLA Modules:
  0.0 2824.1 jit_solution(6068073864397957872)
XLA Ops:
  12.1 53.7 %all-gather.15.cloned.1.call-done = f32[1,32,128,512]{3,2,0,1:T(8,128)} async-done(((f32[1,4,128,512]{3,2,0,1:T(8,128)}), f32[1,32,128,512]{3,2,0,1:T(8,128)}) %all-gather.15.cloned.1.call-update) | async-done | bytes 8388624 | tf_op jit(solution)/shard_map/all_gather | solution.py:61
  74.5 6.1 all-to-all-start.2
  85.8 137.6 %all-gather.17.cloned.1.call-done = f32[1,4,512,512]{2,3,1,0:T(8,128)} async-done(((f32[1,4,128,512]{2,3,1,0:T(8,128)}), f32[1,4,512,512]{2,3,1,0:T(8,128)}) %all-gather.17.cloned.1.call-update) | async-done | bytes 4194320 | tf_op jit(solution)/shard_map/all_gather | solution.py:60
  226.5 60.7 %broadcast_select_fusion.1 = f32[4,512,4096]{2,1,0:T(8,128)} fusion(f32[4,512,4096]{2,1,0:T(8,128)} %bitcast.100, pred[4,4096]{1,0:T(4,128)(4,1)S(1)} %get-tuple-element.19, f32[4,512,512]{1,2,0:T(8,128)S(1)} %bitcast_select_fusion.12), kind=kOutput, calls=%fused_computation.33 | convolution fusion | flops 51547996160 | bytes 71319552 | tf_op jit(solution)/shard_map/kab,kan->kbn/dot_general | solution.py:16
  287.2 37.9 %copy.105 = f32[256,8,8,512]{3,2,1,0:T(8,128)} copy(f32[256,8,8,512]{3,1,2,0:T(8,128)} %bitcast.94) | data formatting | bytes 67108864
  325.1 35.5 %copy.80 = f32[2048,8,512]{0,2,1:T(8,128)} copy(f32[2048,8,512]{2,1,0:T(8,128)} %bitcast.98) | data formatting | bytes 67108864 | tf_op jit(solution)/shard_map/reshape;reshape | solution.py:85
  360.7 18.9 all-to-all-done.2
  379.6 10.0 copy.78
  389.5 10.3 reshape.287
  399.8 63.0 %bitcast_select_fusion.1 = f32[2048,8,512]{0,2,1:T(8,128)} fusion(f32[2048,8,512]{0,2,1:T(8,128)} %copy.80, pred[2048,8]{0,1:T(8,128)(4,1)S(1)} %get-tuple-element.22, f32[8,512,512]{1,2,0:T(8,128)} %reshape.287, f32[512,512]{0,1:T(8,128)S(1)} %fusion.41, pred[8]{0:T(512)(128)(4,1)S(1)} %select_compare_fusion.1), kind=kOutput, calls=%fused_computation.25 | convolution fusion | flops 51550093312 | bytes 76562440 | tf_op jit(solution)/shard_map/nka,kab->nkb/dot_general | solution.py:20
  462.8 39.6 %reshape_reshape.16 = f32[4,512,4096]{1,0,2:T(4,128)} reshape(f32[2048,8,512]{0,2,1:T(8,128)} %bitcast_select_fusion.1) | data formatting | bytes 67108864 | tf_op jit(solution)/shard_map/reshape;reshape | solution.py:78
  502.4 24.2 fusion.50
  526.5 19.2 copy.97
  546.9 19.2 copy.96
  574.2 424.4 %collective-permute-done.1 = f32[4,512,256]{1,2,0:T(8,128)S(1)} collective-permute-done((f32[4,512,256]{1,2,0:T(8,128)}, f32[4,512,256]{1,2,0:T(8,128)S(1)}, u32[]{:S(2)}, u32[]{:S(2)}) %collective-permute-start.1) | collective-permute-done | bytes 2097184 | tf_op jit(solution)/shard_map/ppermute | solution.py:12
  1008.0 53.7 %all-to-all-start.1 = ((f32[1,4,8,128,512]{4,3,2,0,1:T(8,128)}), f32[1,4,8,128,512]{4,3,2,0,1:T(8,128)}, u32[]{:S(2)}, u32[]{:S(2)}) async-start(f32[1,4,8,128,512]{4,3,2,0,1:T(8,128)} %copy.72), calls=%async_computation.1 | async-start | bytes 16777216 | tf_op jit(solution)/shard_map/all_to_all | solution.py:62
  1064.2 10.8 slice.139
  1075.0 16.1 maximum_select_fusion.1
  1091.1 10.8 slice.136
  1104.3 16.1 maximum_select_fusion
  1120.5 38.4 %broadcast_select_fusion.2 = f32[4,256,4096]{2,1,0:T(8,128)} fusion(f32[4,256,4096]{2,1,0:T(8,128)} %copy.96, pred[4,4096]{1,0:T(4,128)(4,1)S(1)} %copy-done.15, f32[4,256,4096]{2,1,0:T(8,128)} %maximum_select_fusion.1, f32[4,512,512]{1,2,0:T(8,128)} %copy-done.7), kind=kOutput, calls=%fused_computation.36 | convolution fusion | flops 25782386688 | bytes 69222400 | tf_op jit(solution)/shard_map/kab,kan->kbn/dot_general | solution.py:16
  1158.9 37.0 %broadcast_select_fusion.3 = f32[4,256,4096]{2,1,0:T(8,128)} fusion(f32[4,256,4096]{2,1,0:T(8,128)} %copy.97, pred[4,4096]{1,0:T(4,128)(4,1)S(1)} %copy-done.14, f32[4,256,4096]{2,1,0:T(8,128)} %maximum_select_fusion, f32[4,512,256]{1,2,0:T(8,128)} %copy-done.8, f32[3,512,256]{1,2,0:T(8,128)S(1)} %slice-done, f32[1,512,256]{1,2,0:T(8,128)S(1)} %slice-done.1, ...), kind=kOutput, calls=%fused_computation.37 | convolution fusion | flops 25783435264 | bytes 54542336 | tf_op jit(solution)/shard_map/kab,kan->kbn/dot_general | solution.py:16
  1195.9 12.8 pad_maximum_fusion
  1208.7 36.7 %copy.106 = f32[256,8,8,512]{3,2,1,0:T(8,128)} copy(f32[256,8,8,512]{3,1,2,0:T(8,128)S(1)} %bitcast.97) | data formatting | bytes 67108864
  1245.4 17.8 fusion.49
  1263.2 15.9 copy.99
  1279.7 10.6 copy.98
  1300.5 8.1 all-to-all-start
  1310.7 10.2 copy.73
  1320.9 10.3 reshape.284
  1345.4 401.6 %all-gather.9.cloned.1.call-done = f32[1,4,512,512]{2,3,1,0:T(8,128)} async-done(((f32[1,4,128,512]{2,3,1,0:T(8,128)}), f32[1,4,512,512]{2,3,1,0:T(8,128)}) %all-gather.9.cloned.1.call-update) | async-done | bytes 4194320 | tf_op jit(solution)/shard_map/all_gather | solution.py:60
  1751.8 582.6 %all-to-all-done = f32[1,4,8,128,512]{4,3,2,0,1:T(8,128)} async-done(((f32[1,4,8,128,512]{4,3,2,0,1:T(8,128)}), f32[1,4,8,128,512]{4,3,2,0,1:T(8,128)}, u32[]{:S(2)}, u32[]{:S(2)}) %all-to-all-start) | async-done | bytes 8388640 | tf_op jit(solution)/shard_map/all_to_all | solution.py:62
  2334.4 9.9 copy.68
  2344.3 10.3 reshape.281
  2361.8 11.8 slice.146
  2373.6 17.1 maximum_select_fusion.3
  2390.8 37.3 %bitcast_select_fusion.2 = f32[2048,8,256]{2,0,1:T(8,128)} fusion(f32[2048,8,256]{2,0,1:T(8,128)} %copy.98, pred[2048,8]{0,1:T(8,128)(4,1)S(1)} %copy-done.17, f32[2048,8,256]{2,0,1:T(8,128)} %maximum_select_fusion.3, f32[8,512,512]{1,2,0:T(8,128)} %copy-done.6), kind=kOutput, calls=%fused_computation.30 | convolution fusion | flops 25782386688 | bytes 71319552 | tf_op jit(solution)/shard_map/nka,kab->nkb/dot_general | solution.py:20
  2428.0 11.8 slice.143
  2441.5 17.1 maximum_select_fusion.2
  2458.7 37.4 %bitcast_select_fusion.3 = f32[2048,8,256]{2,0,1:T(8,128)} fusion(f32[2048,8,256]{2,0,1:T(8,128)} %copy.99, pred[2048,8]{0,1:T(8,128)(4,1)S(1)} %copy-done.16, f32[2048,8,256]{2,0,1:T(8,128)} %maximum_select_fusion.2, f32[8,512,256]{1,2,0:T(8,128)} %collective-permute-done, f32[7,512,256]{1,2,0:T(8,128)} %slice.130, f32[1,512,256]{1,2,0:T(8,128)S(1)} %slice.129, ...), kind=kOutput, calls=%fused_computation.31 | convolution fusion | flops 25784483840 | bytes 58736640 | tf_op jit(solution)/shard_map/nka,kab->nkb/dot_general | solution.py:20
  2496.1 12.9 pad_maximum_fusion.1
  2508.9 43.8 %copy.87 = f32[2048,8,512]{2,1,0:T(8,128)} copy(f32[2048,8,512]{2,0,1:T(8,128)S(1)} %pad_maximum_fusion.1) | data formatting | bytes 67108864 | tf_op jit(solution)/shard_map/concatenate | solution.py:128
  2552.8 35.9 %reshape_reshape.18 = f32[4,512,4096]{2,1,0:T(8,128)} reshape(f32[2048,8,512]{2,1,0:T(8,128)} %copy.87) | data formatting | bytes 67108864 | tf_op jit(solution)/shard_map/reshape;reshape | solution.py:78
  2588.6 61.2 %broadcast_select_fusion = f32[4,512,4096]{2,1,0:T(8,128)} fusion(f32[4,512,4096]{2,1,0:T(8,128)} %reshape_reshape.18, pred[4,4096]{1,0:T(4,128)(4,1)S(1)} %copy-done.12, f32[4,512,512]{1,2,0:T(8,128)} %bitcast_select_fusion.11), kind=kOutput, calls=%fused_computation.32 | convolution fusion | flops 51547996160 | bytes 71319552 | tf_op jit(solution)/shard_map/kab,kan->kbn/dot_general | solution.py:16
  2649.8 37.9 %copy.107 = f32[256,8,8,512]{3,2,1,0:T(8,128)} copy(f32[256,8,8,512]{3,1,2,0:T(8,128)} %bitcast.93) | data formatting | bytes 67108864
  2687.8 35.6 %copy.89 = f32[2048,8,512]{0,2,1:T(8,128)} copy(f32[2048,8,512]{2,1,0:T(8,128)} %bitcast.99) | data formatting | bytes 67108864 | tf_op jit(solution)/shard_map/reshape;reshape | solution.py:85
  2723.4 62.7 %bitcast_select_fusion = f32[2048,8,512]{0,2,1:T(8,128)} fusion(f32[2048,8,512]{0,2,1:T(8,128)} %copy.89, pred[2048,8]{0,1:T(8,128)(4,1)S(1)} %copy-done.10, f32[8,512,512]{1,2,0:T(8,128)} %reshape.281, f32[512,512]{0,1:T(8,128)S(1)} %copy-done.5, pred[8]{0:T(512)(128)(4,1)S(1)} %copy-done.18), kind=kOutput, calls=%fused_computation.24 | convolution fusion | flops 51550093312 | bytes 76562440 | tf_op jit(solution)/shard_map/nka,kab->nkb/dot_general | solution.py:20
  2786.0 31.1 %copy.90 = f32[2048,4096]{1,0:T(8,128)} copy(f32[2048,4096]{0,1:T(8,128)} %bitcast.95) | data formatting | bytes 67108864 | tf_op jit(solution)/shard_map/reshape | solution.py:88
  (124 shorter events, 86.9 us)
Async XLA Ops:
  6.5 59.3 %all-gather.15.cloned.1.call-start = ((), (), s32[]{:S(2)}) async-start(), calls=%async_computation.7 | async-start | bytes 9437184 | tf_op jit(solution)/shard_map/all_gather | solution.py:61
  10.7 212.7 %all-gather.17.cloned.1.call-start = ((), (), s32[]{:S(2)}) async-start(), calls=%async_computation.8 | async-start | bytes 5242880 | tf_op jit(solution)/shard_map/all_gather | solution.py:60
  70.2 12.0 copy-start.21
  74.5 305.1 %all-to-all-start.2 = ((f32[1,4,8,128,512]{4,3,2,0,1:T(8,128)}), f32[1,4,8,128,512]{4,3,2,0,1:T(8,128)}, u32[]{:S(2)}, u32[]{:S(2)}) async-start(f32[1,4,8,128,512]{4,3,2,0,1:T(8,128)} %copy.77), calls=%async_computation.2 | async-start | bytes 16777216 | tf_op jit(solution)/shard_map/all_to_all | solution.py:62
  80.6 486.3 %all-gather.13.cloned.1.call-start = ((), (), s32[]{:S(2)}) async-start(), calls=%async_computation.6 | async-start | bytes 5242880 | tf_op jit(solution)/shard_map/all_gather | solution.py:60
  82.0 916.7 %all-gather.11.cloned.1.call-start = ((), (), s32[]{:S(2)}) async-start(), calls=%async_computation.5 | async-start | bytes 9437184 | tf_op jit(solution)/shard_map/all_gather | solution.py:61
  82.2 2.9 copy-start.19
  83.4 1.7 copy-start.20
  84.2 482.8 %copy-start.3 = (f32[512,512]{0,1:T(8,128)}, f32[512,512]{0,1:T(8,128)S(1)}, u32[]{:S(2)}) copy-start(f32[512,512]{0,1:T(8,128)S(1)} %fusion.41) | copy-start | bytes 3145732
  85.1 314.7 %copy-start.9 = (pred[2048,8]{0,1:T(8,128)(4,1)}, pred[2048,8]{0,1:T(8,128)(4,1)S(1)}, u32[]{:S(2)}) copy-start(pred[2048,8]{0,1:T(8,128)(4,1)S(1)} %get-tuple-element.22) | copy-start | bytes 49156
  85.8 201.4 %copy-start.11 = (pred[4,4096]{1,0:T(4,128)(4,1)}, pred[4,4096]{1,0:T(4,128)(4,1)S(1)}, u32[]{:S(2)}) copy-start(pred[4,4096]{1,0:T(4,128)(4,1)S(1)} %get-tuple-element.19) | copy-start | bytes 49156
  545.7 516.0 %collective-permute-start.3 = (f32[4,256,4096]{2,1,0:T(8,128)}, f32[4,256,4096]{2,1,0:T(8,128)}, u32[]{:S(2)}, u32[]{:S(2)}) collective-permute-start(f32[4,256,4096]{2,1,0:T(8,128)} %copy.97), channel_id=1, source_target_pairs={{0,28},{4,0},{8,4},{12,8},{16,12},{20,16},{24,20},{28,24},{1,29},{... | collective-permute-start | bytes 50331656 | tf_op jit(solution)/shard_map/ppermute | solution.py:12
  546.9 19.3 copy-start.1
  566.1 525.0 %collective-permute-start.2 = (f32[4,256,4096]{2,1,0:T(8,128)}, f32[4,256,4096]{2,1,0:T(8,128)}, u32[]{:S(2)}, u32[]{:S(2)}) collective-permute-start(f32[4,256,4096]{2,1,0:T(8,128)} %copy.96), channel_id=1, source_target_pairs={{0,4},{4,8},{8,12},{12,16},{16,20},{20,24},{24,28},{28,0},{1,5},{5... | collective-permute-start | bytes 50331656 | tf_op jit(solution)/shard_map/ppermute | solution.py:12
  566.1 725.7 %all-gather.7.cloned.1.call-start = ((), (), s32[]{:S(2)}) async-start(), calls=%async_computation.3 | async-start | bytes 9437184 | tf_op jit(solution)/shard_map/all_gather | solution.py:61
  569.9 2.0 copy-start.7
  573.4 425.2 %collective-permute-start.1 = (f32[4,512,256]{1,2,0:T(8,128)}, f32[4,512,256]{1,2,0:T(8,128)S(1)}, u32[]{:S(2)}, u32[]{:S(2)}) collective-permute-start(f32[4,512,256]{1,2,0:T(8,128)} %slice.131), channel_id=1, source_target_pairs={{0,4},{4,8},{8,12},{12,16},{16,20},{20,24},{24,28},{28,0},{1,5},{5... | collective-permute-start | bytes 6291464 | tf_op jit(solution)/shard_map/ppermute | solution.py:12
  998.6 9.4 copy-start.8
  1008.0 292.4 %all-to-all-start.1 = ((f32[1,4,8,128,512]{4,3,2,0,1:T(8,128)}), f32[1,4,8,128,512]{4,3,2,0,1:T(8,128)}, u32[]{:S(2)}, u32[]{:S(2)}) async-start(f32[1,4,8,128,512]{4,3,2,0,1:T(8,128)} %copy.72), calls=%async_computation.1 | async-start | bytes 16777216 | tf_op jit(solution)/shard_map/all_to_all | solution.py:62
  1104.3 16.1 copy-start.15
  1120.5 38.4 %slice-start = ((f32[4,512,256]{1,2,0:T(8,128)}), f32[3,512,256]{1,2,0:T(8,128)S(1)}, s32[]{:S(2)}) async-start(f32[4,512,256]{1,2,0:T(8,128)} %copy-done.8), calls=%async_computation.9 | async-start | bytes 3145728 | tf_op jit(solution)/shard_map/jit(_roll_static)/slice | solution.py:29
  1120.5 38.4 %slice-start.1 = ((f32[4,512,256]{1,2,0:T(8,128)}), f32[1,512,256]{1,2,0:T(8,128)S(1)}, s32[]{:S(2)}) async-start(f32[4,512,256]{1,2,0:T(8,128)} %copy-done.8), calls=%async_computation.10 | async-start | bytes 1048576 | tf_op jit(solution)/shard_map/jit(_roll_static)/slice | solution.py:29
  1120.5 38.4 %copy-start.14 = (pred[4,4096]{1,0:T(4,128)(4,1)S(1)}, pred[4,4096]{1,0:T(4,128)(4,1)}, u32[]{:S(2)}) copy-start(pred[4,4096]{1,0:T(4,128)(4,1)} %get-tuple-element.17) | copy-start | bytes 49156
  1279.1 1080.9 %collective-permute-start.5 = (f32[2048,8,256]{2,0,1:T(8,128)}, f32[2048,8,256]{2,0,1:T(8,128)}, u32[]{:S(2)}, u32[]{:S(2)}) collective-permute-start(f32[2048,8,256]{2,0,1:T(8,128)} %copy.99), channel_id=1, source_target_pairs={{0,3},{1,0},{2,1},{3,2},{4,7},{5,4},{6,5},{7,6},{8,11},{9,8},{10,9... | collective-permute-start | bytes 50331656 | tf_op jit(solution)/shard_map/ppermute | solution.py:12
  1290.3 1137.7 %collective-permute-start.4 = (f32[2048,8,256]{2,0,1:T(8,128)}, f32[2048,8,256]{2,0,1:T(8,128)}, u32[]{:S(2)}, u32[]{:S(2)}) collective-permute-start(f32[2048,8,256]{2,0,1:T(8,128)} %copy.98), channel_id=1, source_target_pairs={{0,1},{1,2},{2,3},{3,0},{4,5},{5,6},{6,7},{7,4},{8,9},{9,10},{10,1... | collective-permute-start | bytes 50331656 | tf_op jit(solution)/shard_map/ppermute | solution.py:12
  1296.2 12.4 copy-start.13
  1296.2 13.8 copy-start.2
  1300.5 1033.9 %all-to-all-start = ((f32[1,4,8,128,512]{4,3,2,0,1:T(8,128)}), f32[1,4,8,128,512]{4,3,2,0,1:T(8,128)}, u32[]{:S(2)}, u32[]{:S(2)}) async-start(f32[1,4,8,128,512]{4,3,2,0,1:T(8,128)} %copy.67), calls=%async_computation | async-start | bytes 16777216 | tf_op jit(solution)/shard_map/all_to_all | solution.py:62
  1308.6 438.4 %all-gather.9.cloned.1.call-start = ((), (), s32[]{:S(2)}) async-start(), calls=%async_computation.4 | async-start | bytes 5242880 | tf_op jit(solution)/shard_map/all_gather | solution.py:60
  1310.7 20.5 copy-start.4
  1331.2 12.1 copy-start
  1335.8 3.4 copy-start.6
  1341.7 1012.9 %collective-permute-start = (f32[8,512,256]{1,2,0:T(8,128)}, f32[8,512,256]{1,2,0:T(8,128)}, u32[]{:S(2)}, u32[]{:S(2)}) collective-permute-start(f32[8,512,256]{1,2,0:T(8,128)} %slice.128), channel_id=1, source_target_pairs={{0,1},{1,2},{2,3},{3,0},{4,5},{5,6},{6,7},{7,4},{8,9},{9,10},{10,1... | collective-permute-start | bytes 12582920 | tf_op jit(solution)/shard_map/ppermute | solution.py:12
  2373.6 17.1 copy-start.17
  2441.5 17.2 copy-start.16
  2552.8 35.9 %copy-start.12 = (pred[4,4096]{1,0:T(4,128)(4,1)S(1)}, pred[4,4096]{1,0:T(4,128)(4,1)}, u32[]{:S(2)}) copy-start(pred[4,4096]{1,0:T(4,128)(4,1)} %copy-done.11) | copy-start | bytes 49156
  2687.8 35.6 %copy-start.5 = (f32[512,512]{0,1:T(8,128)S(1)}, f32[512,512]{0,1:T(8,128)}, u32[]{:S(2)}) copy-start(f32[512,512]{0,1:T(8,128)} %copy-done.3) | copy-start | bytes 3145732
  2687.8 35.6 %copy-start.10 = (pred[2048,8]{0,1:T(8,128)(4,1)S(1)}, pred[2048,8]{0,1:T(8,128)(4,1)}, u32[]{:S(2)}) copy-start(pred[2048,8]{0,1:T(8,128)(4,1)} %copy-done.9) | copy-start | bytes 49156
  2687.8 35.6 %copy-start.18 = (pred[8]{0:T(512)(128)(4,1)S(1)}, pred[8]{0:T(512)(128)(4,1)}, u32[]{:S(2)}) copy-start(pred[8]{0:T(512)(128)(4,1)} %select_compare_fusion.3) | copy-start | bytes 28
Sparse Core Ops, SparseCore 0:
  10.8 54.9 all-gather.14
  67.3 156.0 all-gather.16
  225.0 170.3 all-gather.12
  566.2 137.5 all-gather.10
  705.6 87.2 all-gather.6
  1310.6 436.3 all-gather.8
where the time goes:
time: 2830 us; the launch traced here: 2820 us
  waiting for transfers between devices  1620 us (57%)
  local copies, waits for them, and re-layouts  610 us (22%)
  matrix products  398 us (14%)
  other arithmetic  110 us (4%)
  starting transfers between devices  73.7 us (3%)
    all_to_all x3, waiting for transfers between devices, local(): lax.all_to_all(sort_columns(gathered, grid_rows, grid_cols, col_blocks),...  601 us
    all_gather x3, waiting for transfers between devices, local(): row_raw = lax.all_gather(chosen, 'col', axis=2, tiled=True)[0]  539 us
    ppermute x6, waiting for transfers between devices, passed_along(): return lax.ppermute(value, axis, pairs)  424 us
    dot_general x4, matrix products, right_apply(): return jnp.einsum('nka,kab->nkb', stacked, factor, precision=PRECISE)  200 us
    dot_general x4, matrix products, left_apply(): return jnp.einsum('kab,kan->kbn', factor, stacked, precision=PRECISE)  197 us
    unnamed x56, local copies, waits for them, and re-layouts  187 us
    another operation x2, local copies, waits for them, and re-layouts, local(): blocks = current.reshape(row_blocks, window, cols_here)  75.4 us
    another operation x2, local copies, waits for them, and re-layouts, local(): columns = current.reshape(rows_here, col_blocks, window)  71.1 us
  transfers between devices with their start and end apart: 15, of which 6 were waited for; matrix products, arithmetic and copies ran while one was open for 25% of the time, Pallas kernels for 0%

commit v1 on v0

v1 whole, which is shorter than its diff:
```python
import jax
import jax.numpy as jnp
from jax import lax
from jax.experimental import pallas as pl
from jax.experimental.pallas import tpu as pltpu
from jax.sharding import PartitionSpec as P


F32 = jnp.float32
BF16 = jnp.bfloat16


def split(x):
    hi = x.astype(BF16)
    return hi, (x - hi.astype(F32)).astype(BF16)


def mul(left, right):
    (lh, ll), (rh, rl) = left, right
    return lax.dot_general(
        jnp.concatenate([lh, lh, ll], axis=1),
        jnp.concatenate([rh, rl, rh], axis=0),
        (((1,), (0,)), ((), ())),
        preferred_element_type=F32,
    )


def call(kernel, grid, in_specs, out_specs, out_shape, scratch, flops, moved, aliases=None):
    return pl.pallas_call(
        kernel,
        grid_spec=pltpu.PrefetchScalarGridSpec(
            num_scalar_prefetch=1,
            grid=(grid,),
            in_specs=in_specs,
            out_specs=out_specs,
            scratch_shapes=scratch,
        ),
        out_shape=out_shape,
        input_output_aliases=aliases or {},
        cost_estimate=pl.CostEstimate(
            flops=int(flops), bytes_accessed=int(moved), transcendentals=0
        ),
    )


def shape(dims, dtype=F32):
    return jax.ShapeDtypeStruct(dims, dtype)


class Plan:
    def __init__(self, rows, cols, win, grid_rows, grid_cols):
        self.win, self.half = win, win // 2
        self.R, self.C = grid_rows, grid_cols
        self.kb, self.mb = rows // win, cols // win
        self.N = self.kb * grid_rows
        self.t = grid_rows // grid_cols
        assert grid_rows % grid_cols == 0 and grid_rows & (grid_rows - 1) == 0

    def first(self, k):
        return k * self.t

    def count(self, k):
        return self.mb - k * self.t


def ring(value, axis, steps):
    size = lax.axis_size(axis)
    return lax.ppermute(value, axis, [(s, (s + steps) % size) for s in range(size)])


def along(value, axis, steps):
    size = lax.axis_size(axis)
    pairs = [(s, s + steps) for s in range(size) if 0 <= s + steps < size]
    return lax.ppermute(value, axis, pairs)


def around(value, axis, steps):
    last = lax.axis_size(axis) - 1
    return lax.ppermute(value, axis, [(last, 0) if steps > 0 else (0, last)])


def swap(value, axis, bit):
    size = lax.axis_size(axis)
    return lax.ppermute(value, axis, [(s, s ^ bit) for s in range(size)])


def flag(s, g, phase, slot):
    return s[2 + phase * g.N + jnp.clip(slot, 0, g.N - 1)] > 0


def column_factors(g, scalars, same, other):
    part = g.win // g.C

    def kernel(s, same_ref, other_ref, hi, lo):
        for at in range(g.R):
            h, z = at // g.C, at % g.C
            spot = s[0] ^ at
            hi_part, lo_part = split(
                jnp.where(spot % 2 == 0, same_ref[spot // 2, 0], other_ref[spot // 2, 0])
            )
            hi[h, z * part : (z + 1) * part, :] = hi_part
            lo[h, z * part : (z + 1) * part, :] = lo_part

    size = g.mb * g.win * g.win * 4
    return call(
        kernel,
        g.kb,
        [pl.BlockSpec((g.R // 2, 1, part, g.win), lambda i, s: (0, i, 0, 0))] * 2,
        [pl.BlockSpec((g.t, g.win, g.win), lambda i, s: (i, 0, 0))] * 2,
        [shape((g.mb, g.win, g.win), BF16)] * 2,
        [],
        size,
        2 * size,
    )(scalars, same, other)


def keep_lower(g, matrix):
    W = g.win
    spots = [(k, m) for k in range(g.kb) for m in range(g.first(k))]
    if not spots:
        return matrix + 0.0

    def kernel(s, h_ref, o_ref):
        o_ref[...] = h_ref[...]

    block = pl.BlockSpec((W, W), lambda i, s: (s[2 * i], s[2 * i + 1]))
    size = len(spots) * W * W
    return call(
        kernel, len(spots), [block], block, shape(matrix.shape), [], size, 8 * size
    )(jnp.asarray(spots, jnp.int32).reshape(-1), matrix)


def even_first(g, k, scalars, matrix, row_factor, col_hi, col_lo):
    W, half, lo_m, n = g.win, g.half, g.first(k), g.count(k)

    def kernel(s, h_ref, q_ref, ch, cl, left, later, right, qh, ql, x):
        i = pl.program_id(0)
        r, c = k * g.R + s[0], (lo_m + i) * g.C + s[1]
        upper = c > r

        @pl.when(i == 0)
        def _():
            qh[...], ql[...] = split(q_ref[0].T)

        do_left = upper & flag(s, g, 0, r)
        do_right = upper & flag(s, g, 0, c)

        @pl.when(do_left)
        def _():
            x[...] = mul((qh[...], ql[...]), split(h_ref[...]))

        @pl.when(jnp.logical_not(do_left))
        def _():
            x[...] = h_ref[...]

        @pl.when(do_right)
        def _():
            y = mul(split(x[...]), (ch[0], cl[0]))
            left[0] = y[:, :half]
            right[0] = y[:, half:]

            @pl.when(i > 0)
            def _():
                later[0] = y[:, :half]

        @pl.when(jnp.logical_not(do_right))
        def _():
            left[0] = x[:, :half]
            right[0] = x[:, half:]

            @pl.when(i > 0)
            def _():
                later[0] = x[:, :half]

    return call(
        kernel,
        n,
        [
            pl.BlockSpec((W, W), lambda i, s: (k, lo_m + i)),
            pl.BlockSpec((1, W, W), lambda i, s: (k, 0, 0)),
            pl.BlockSpec((1, W, W), lambda i, s: (lo_m + i, 0, 0)),
            pl.BlockSpec((1, W, W), lambda i, s: (lo_m + i, 0, 0)),
        ],
        [
            pl.BlockSpec((1, W, half), lambda i, s: (i, 0, 0)),
            pl.BlockSpec((1, W, half), lambda i, s: (jnp.maximum(i - 1, 0), 0, 0)),
            pl.BlockSpec((1, W, half), lambda i, s: (i, 0, 0)),
        ],
        [shape((n, W, half)), shape((max(n - 1, 1), W, half)), shape((n, W, half))],
        [pltpu.VMEM((W, W), BF16), pltpu.VMEM((W, W), BF16), pltpu.VMEM((W, W), F32)],
        12 * n * W**3,
        12 * n * W * W,
    )(scalars, matrix, row_factor, col_hi, col_lo)


def odd_right(g, k, scalars, right, beyond, round_end, col_hi, col_lo):
    W, half, lo_m, n = g.win, g.half, g.first(k), g.count(k)
    few = max(n - 1, 1)

    def kernel(s, r_ref, b_ref, e_ref, ch, cl, lt, lb, lt_end, lb_end, rt, rb):
        i = pl.program_id(0)
        r, c = k * g.R + s[0], (lo_m + i) * g.C + s[1]
        at_end = s[1] == g.C - 1
        do = (c < g.N - 1) & (r <= c) & flag(s, g, 1, c)

        def theirs(rows):
            return jnp.where(at_end, e_ref[0, rows], b_ref[0, rows])

        @pl.when(do)
        def _():
            x = jnp.concatenate([r_ref[0], theirs(slice(0, W))], axis=1)
            y = mul(split(x), (ch[0], cl[0]))
            rt[0] = y[:half, :half]
            lt[0] = y[:half, half:]
            rb[0] = y[half:, :half]
            lb[0] = y[half:, half:]

        @pl.when(jnp.logical_not(do))
        def _():
            rt[0] = r_ref[0, :half]
            lt[0] = theirs(slice(0, half))

        @pl.when(jnp.logical_not(do) | (r == c))
        def _():
            rb[0] = r_ref[0, half:]
            lb[0] = theirs(slice(half, W))

        @pl.when(i < few)
        def _():
            lt_end[0] = lt[0]
            lb_end[0] = lb[0]

    whole = pl.BlockSpec((1, half, half), lambda i, s: (i, 0, 0))
    part = pl.BlockSpec((1, half, half), lambda i, s: (jnp.minimum(i, few - 1), 0, 0))
    return call(
        kernel,
        n,
        [
            pl.BlockSpec((1, W, half), lambda i, s: (i, 0, 0)),
            pl.BlockSpec((1, W, half), lambda i, s: (jnp.where(s[1] == g.C - 1, 0, i), 0, 0)),
            pl.BlockSpec(
                (1, W, half),
                lambda i, s: (jnp.where(s[1] == g.C - 1, jnp.minimum(i, few - 1), 0), 0, 0),
            ),
            pl.BlockSpec((1, W, W), lambda i, s: (lo_m + i, 0, 0)),
            pl.BlockSpec((1, W, W), lambda i, s: (lo_m + i, 0, 0)),
        ],
        [whole, whole, part, part, whole, whole],
        [shape((m, half, half)) for m in (n, n, few, few, n, n)],
        [],
        6 * n * W**3,
        12 * n * W * W,
    )(scalars, right, beyond, round_end, col_hi, col_lo)


def finish(g, k, scalars, matrix, factors, col_hi, col_lo, own, below, above, out):
    W, half, lo_m, n = g.win, g.half, g.first(k), g.count(k)
    this, prior, last = factors

    def spec(source, wanted=None):
        size, start = g.count(source), g.first(source)

        def index(i, s):
            at = jnp.clip(lo_m + i - start, 0, size - 1)
            if wanted is not None:
                at = jnp.where(wanted(s), at, 0)
            return (at, 0, 0)

        return pl.BlockSpec((1, half, half), index)

    bottom_edge = lambda s: s[0] == g.R - 1
    top_edge = lambda s: s[0] == 0
    has_next, has_prev = below[1] is not None, above[1] is not None

    def kernel(s, h_ref, q1, qp, q2, ch, cl, lt, lb, rt, rb, *rest):
        rest = list(rest)
        take = lambda: (rest.pop(0), rest.pop(0))
        below_here, above_here = take(), take()
        below_next = take() if has_next else below_here
        above_prev = take() if has_prev else above_here
        rest.pop(0)
        o_ref, bh, bl, th, tl, qh, ql, x = rest
        i = pl.program_id(0)
        r, c = k * g.R + s[0], (lo_m + i) * g.C + s[1]

        @pl.when(i == 0)
        def _():
            bh[...], bl[...] = split(q1[0].T[:half])
            th[...], tl[...] = split(qp[0].T)
            qh[...], ql[...] = split(q2[0].T)

        @pl.when(c < r)
        def _():
            o_ref[...] = h_ref[...]

        @pl.when(c >= r)
        def _():
            x[:half, :half] = lt[0]
            x[:half, half:] = rt[0]
            x[half:, :half] = lb[0]
            x[half:, half:] = rb[0]
            do_top = (r > 0) & flag(s, g, 1, r - 1)
            do_bottom = (r < g.N - 1) & (c > r) & flag(s, g, 1, r)

            def top(pair):
                upper = jnp.concatenate([pair[0][0], pair[1][0]], axis=1)
                lower = jnp.concatenate([lt[0], rt[0]], axis=1)
                y = mul((th[...], tl[...]), split(jnp.concatenate([upper, lower], axis=0)))
                x[:half, :] = y

            def bottom(pair):
                upper = jnp.concatenate([lb[0], rb[0]], axis=1)
                lower = jnp.concatenate([pair[0][0], pair[1][0]], axis=1)
                y = mul((bh[...], bl[...]), split(jnp.concatenate([upper, lower], axis=0)))
                x[half:, half:] = y[:, half:]

                @pl.when(c > r + 1)
                def _():
                    x[half:, :half] = y[:, :half]

            edge = top_edge(s)
            if has_prev:
                pl.when(do_top & edge)(lambda: top(above_prev))
            pl.when(do_top & jnp.logical_not(edge))(lambda: top(above_here))
            edge = bottom_edge(s)
            if has_next:
                pl.when(do_bottom & edge)(lambda: bottom(below_next))
            pl.when(do_bottom & jnp.logical_not(edge))(lambda: bottom(below_here))

            @pl.when(c == r)
            def _():
                x[:, :half] = h_ref[:, :half]

            @pl.when((c > r) & flag(s, g, 2, r))
            def _():
                x[...] = mul((qh[...], ql[...]), split(x[...]))

            do_right = (c > r) & flag(s, g, 2, c)

            @pl.when(do_right)
            def _():
                o_ref[...] = mul(split(x[...]), (ch[0], cl[0]))

            @pl.when(jnp.logical_not(do_right))
            def _():
                o_ref[...] = x[...]

    const = lambda i, s: (k, 0, 0)
    column = pl.BlockSpec((1, W, W), lambda i, s: (lo_m + i, 0, 0))
    operands = [matrix, this, prior, last, col_hi, col_lo, *own, *below[0], *above[0]]
    in_specs = [
        pl.BlockSpec((W, W), lambda i, s: (k, lo_m + i)),
        pl.BlockSpec((1, W, W), const),
        pl.BlockSpec(
            (1, W, half),
            lambda i, s: (jnp.maximum(k - jnp.where(s[0] == 0, 1, 0), 0), 0, 0),
        ),
        pl.BlockSpec((1, W, W), const),
        column,
        column,
        spec(k),
        spec(k),
        spec(k),
        spec(k),
        spec(k),
        spec(k),
        spec(k),
        spec(k),
    ]
    if has_next:
        operands += below[1]
        in_specs += [spec(k + 1, bottom_edge), spec(k + 1, bottom_edge)]
    if has_prev:
        operands += above[1]
        in_specs += [spec(k - 1, top_edge), spec(k - 1, top_edge)]
    aliases = {1 + len(operands): 0}
    operands.append(out)
    in_specs.append(pl.BlockSpec(memory_space=pl.ANY))
    return call(
        kernel,
        n,
        in_specs,
        pl.BlockSpec((W, W), lambda i, s: (k, lo_m + i)),
        shape(matrix.shape),
        [pltpu.VMEM((half, W), BF16)] * 4
        + [pltpu.VMEM((W, W), BF16)] * 2
        + [pltpu.VMEM((W, W), F32)],
        18 * n * W**3,
        24 * n * W * W,
        aliases,
    )(scalars, *operands)


def local(hessenberg, factors, active):
    rows_here, cols_here = hessenberg.shape
    phases, _, _, win = factors.shape
    R, C = lax.axis_size("row"), lax.axis_size("col")
    g = Plan(rows_here, cols_here, win, R, C)
    assert phases == 3
    p, q = lax.axis_index("row"), lax.axis_index("col")
    scalars = jnp.concatenate(
        [jnp.stack([p, q]).astype(jnp.int32), active.astype(jnp.int32).reshape(-1)]
    )

    spread = [
        [
            ((h * C + a) * C + a, (h * C + (a + d) % C) * C + a)
            for h in range(g.t)
            for a in range(C)
        ]
        for d in range(C)
    ]
    part = g.win // C

    row_factor, col_factor = [], []
    for f in range(phases):
        row_factor.append(lax.all_gather(factors[f], "col", axis=1, tiled=True))
        cut = [
            lax.dynamic_slice_in_dim(row_factor[f], (q + d) % C * part, part, axis=1)
            for d in range(C)
        ]
        piece = jnp.where(p % C == q, cut[0], 0.0)
        for d in range(1, C):
            piece = piece + lax.ppermute(cut[d], ("row", "col"), spread[d])
        same = [piece]
        for j in range(2, R, 2):
            same.append(swap(piece, "row", j))
        same = jnp.stack(same)
        other = swap(same, "row", 1)
        col_factor.append(column_factors(g, scalars, same, other))
    prior = ring(row_factor[1][:, :, g.half :], "row", 1)

    own, tops, bottoms = [], [], []
    for k in range(g.kb):
        left, later, right = even_first(g, k, scalars, hessenberg, row_factor[0], *col_factor[0])
        beyond = along(left, "col", -1)
        round_end = around(later, "col", -1)
        lt, lb, lt_end, lb_end, rt, rb = odd_right(
            g, k, scalars, right, beyond, round_end, *col_factor[1]
        )
        lt = along(lt, "col", 1)
        lb = along(lb, "col", 1)
        lt_end = around(lt_end, "col", 1)
        lb_end = around(lb_end, "col", 1)
        lt, lb = joined(lt, lt_end), joined(lb, lb_end)
        own.append((lt, lb, rt, rb))
        rt = ring(rt, "row", -1)
        rb = ring(rb, "row", 1)
        lt = ring(lt, "row", -1)
        lb = ring(lb, "row", 1)
        tops.append((lt, rt))
        bottoms.append((lb, rb))
    out = keep_lower(g, hessenberg)
    for k in range(g.kb):
        below = (tops[k], tops[k + 1] if k + 1 < g.kb else None)
        above = (bottoms[k], bottoms[k - 1] if k > 0 else None)
        out = finish(
            g,
            k,
            scalars,
            hessenberg,
            (row_factor[1], prior, row_factor[2]),
            *col_factor[2],
            own[k],
            below,
            above,
            out,
        )
    return out


def joined(straight, end):
    extra = straight.shape[0] - 1
    if not extra:
        return straight
    return straight + jnp.pad(end, ((1, 0), (0, 0), (0, 0)))


def solution(mesh):
    return jax.shard_map(
        local,
        mesh=mesh,
        in_specs=(P("row", "col"), P(None, "row", "col", None), P()),
        out_specs=P("row", "col"),
        check_vma=False,
    )
```

time: 2830 us -> 1110 us (0.39)
  waiting for transfers between devices: 1620 us -> 615 us
  local copies, waits for them, and re-layouts: 610 us -> 19.9 us
  matrix products: 398 us -> 0 us
  Pallas kernels: 0 us -> 190 us
  starting transfers between devices: 73.7 us -> 215 us
  other arithmetic: 110 us -> 31.8 us
    all_to_all x3 -> x0, waiting for transfers between devices: 601 us -> none  [local(): lax.all_to_all(sort_columns(gathered, grid_rows, grid_cols, col_blocks),...]
    dot_general x8 -> x0, matrix products: 398 us -> none  [the longest x4 200 us: right_apply(): return jnp.einsum('nka,kab->nkb', stacked, factor, precision=PRECISE)]
    all_gather x6 -> x3, waiting for transfers between devices: 593 us -> 218 us  [local(): row_factor.append(lax.all_gather(factors[f], 'col', axis=1, tiled=True))]
    ppermute x6 -> x62, starting transfers between devices: 5.67 us -> 215 us  [the longest x12 126 us: along(): return lax.ppermute(value, axis, pairs)]
    pallas_call x0 -> x16, Pallas kernels: none -> 190 us  [the longest x4 63.5 us: finish(): call(kernel, n, in_specs, pl.BlockSpec((W, W), lambda i, s: (k, lo_m + i)...]
    unnamed x56 -> x42, local copies, waits for them, and re-layouts: 187 us -> 3.53 us
    another operation x4 -> x0, local copies, waits for them, and re-layouts: 147 us -> none  [the longest x2 75.4 us: local(): blocks = current.reshape(row_blocks, window, cols_here)]
    slice x19 -> x2, local copies, waits for them, and re-layouts: 109 us -> 6.64 us  [the longest x1 3.59 us: local(): row_factor.append(lax.all_gather(factors[f], 'col', axis=1, tiled=True))]
  transfers between devices with their start and end apart: 15 -> 65, of which waited for: 6 -> 17; matrix products, arithmetic and copies ran while one was open for 25% -> 4% of each run, Pallas kernels for 0% -> 17%
where the time goes in v1:
time: 1110 us; the launch traced here: 1090 us
  waiting for transfers between devices  615 us (55%)
  starting transfers between devices  215 us (19%)
  Pallas kernels  190 us (17%)
  other arithmetic  31.8 us (3%)
  local copies, waits for them, and re-layouts  19.9 us (2%)
  between operations  14 us (1%)
    ppermute x12, waiting for transfers between devices, along(): return lax.ppermute(value, axis, pairs)  241 us
    all_gather x3, waiting for transfers between devices, local(): row_factor.append(lax.all_gather(factors[f], 'col', axis=1, tiled=True))  218 us
    ppermute x12, starting transfers between devices, along(): return lax.ppermute(value, axis, pairs)  126 us
    ppermute x17, waiting for transfers between devices, ring(): lax.ppermute(value, axis, [(s, (s + steps) % size) for s in range(size)])  69.6 us
    pallas_call x4, Pallas kernels, finish(): call(kernel, n, in_specs, pl.BlockSpec((W, W), lambda i, s: (k, lo_m + i)...  63.5 us
    ppermute x12, waiting for transfers between devices, swap(): return lax.ppermute(value, axis, [(s, s ^ bit) for s in range(size)])  62.4 us
    pallas_call x4, Pallas kernels, even_first(): call(kernel, n, [pl.BlockSpec((W, W), lambda i, s: (k, lo_m + i)), pl.Blo...  47.7 us
    pallas_call x4, Pallas kernels, odd_right(): call(kernel, n, [pl.BlockSpec((1, W, half), lambda i, s: (i, 0, 0)), pl.B...  40.5 us
  transfers between devices with their start and end apart: 65, of which 17 were waited for; matrix products, arithmetic and copies ran while one was open for 4% of the time, Pallas kernels for 17%

profile of v1, /device:TPU:20, one launch (start us, length us, event | category | flops | bytes accessed | tf_op | source)
XLA Modules:
  0.0 1085.8 jit_solution(7925419741579490487)
XLA Ops:
  11.7 78.9 %all-gather.11.cloned.1.call-done = f32[1,4,512,512]{3,2,1,0:T(8,128)} async-done(((f32[1,4,128,512]{3,2,1,0:T(8,128)}), f32[1,4,512,512]{3,2,1,0:T(8,128)}) %all-gather.11.cloned.1.call-update) | async-done | bytes 4194320 | tf_op jit(solution)/shard_map/all_gather | solution.py:417
  90.6 3.6 dynamic-slice_bitcast_fusion.5
  97.9 73.5 %all-gather.7.cloned.1.call-done = f32[1,4,512,512]{3,2,1,0:T(8,128)} async-done(((f32[1,4,128,512]{3,2,1,0:T(8,128)}), f32[1,4,512,512]{3,2,1,0:T(8,128)}) %all-gather.7.cloned.1.call-update) | async-done | bytes 4194320 | tf_op jit(solution)/shard_map/all_gather | solution.py:417
  171.4 3.7 dynamic-slice_bitcast_fusion.2
  180.7 4.2 collective-permute-start.13
  186.4 65.8 %all-gather.9.cloned.1.call-done = f32[1,4,512,512]{3,2,1,0:T(8,128)} async-done(((f32[1,4,128,512]{3,2,1,0:T(8,128)}), f32[1,4,512,512]{3,2,1,0:T(8,128)}) %all-gather.9.cloned.1.call-update) | async-done | bytes 4194320 | tf_op jit(solution)/shard_map/all_gather | solution.py:417
  264.1 4.5 pad_maximum_fusion.1.same_ref
  268.6 12.8 %collective-permute-start.20 = (f32[4,128,512]{2,1,0:T(8,128)S(1)}, f32[4,128,512]{2,1,0:T(8,128)S(1)}, u32[]{:S(2)}, u32[]{:S(2)}) collective-permute-start(f32[4,128,512]{2,1,0:T(8,128)S(1)} %fusion.1), channel_id=1, source_target_pairs={{0,8},{4,12},{8,0},{12,4},{16,24},{20,28},{24,16},{28,20},{1,9},{5... | collective-permute-start | bytes 3145736 | tf_op jit(solution)/shard_map/ppermute | solution.py:84
  281.4 22.7 %collective-permute-done.2 = f32[4,128,512]{2,1,0:T(8,128)S(1)} collective-permute-done((f32[4,128,512]{2,1,0:T(8,128)S(1)}, f32[4,128,512]{2,1,0:T(8,128)S(1)}, u32[]{:S(2)}, u32[]{:S(2)}) %collective-permute-start.2) | collective-permute-done | bytes 1048608 | tf_op jit(solution)/shard_map/ppermute | solution.py:424
  305.9 20.1 %collective-permute-done.22 = f32[4,128,512]{2,1,0:T(8,128)S(1)} collective-permute-done((f32[4,128,512]{2,1,0:T(8,128)S(1)}, f32[4,128,512]{2,1,0:T(8,128)S(1)}, u32[]{:S(2)}, u32[]{:S(2)}) %collective-permute-start.22) | collective-permute-done | bytes 1048608 | tf_op jit(solution)/shard_map/ppermute | solution.py:84
  328.1 20.9 %collective-permute-done.20 = f32[4,128,512]{2,1,0:T(8,128)S(1)} collective-permute-done((f32[4,128,512]{2,1,0:T(8,128)S(1)}, f32[4,128,512]{2,1,0:T(8,128)S(1)}, u32[]{:S(2)}, u32[]{:S(2)}) %collective-permute-start.20) | collective-permute-done | bytes 1048608 | tf_op jit(solution)/shard_map/ppermute | solution.py:84
  351.7 10.1 collective-permute-done.6
  361.8 11.2 %collective-permute-done.4 = f32[4,128,512]{2,1,0:T(8,128)S(1)} collective-permute-done((f32[4,128,512]{2,1,0:T(8,128)S(1)}, f32[4,128,512]{2,1,0:T(8,128)S(1)}, u32[]{:S(2)}, u32[]{:S(2)}) %collective-permute-start.4) | collective-permute-done | bytes 1048608 | tf_op jit(solution)/shard_map/ppermute | solution.py:84
  380.0 8.0 shard_map.47
  388.0 6.4 shard_map.48
  398.3 18.1 %shard_map.55 = (f32[8,512,256]{2,1,0:T(8,128)}, f32[7,512,256]{2,1,0:T(8,128)}, f32[8,512,256]{2,1,0:T(8,128)}) custom-call(s32[98]{0:T(128)} %pad_add_fusion.8.s, f32[2048,4096]{1,0:T(8,128)} %h_ref.17, f32[4,512,512]{2,1,0:T(8,128)} %bitcast.63, bf16[8,512,512]{2,1,0:T(8,128)(2,1)} %get-tuple-element.49.ch, bf16[8,512,512]{2,1,0:T(8,128)(2,1)} %get-tuple-element.50.cl), custom_call_target="tpu_custom_call" | custom-call | flops 12884901888 | bytes 25165824 | tf_op jit(solution)/shard_map/pallas_call | solution.py:175
  416.4 8.0 shard_map.49
  425.5 5.2 shard_map.50
  431.5 10.7 shard_map.51
  446.5 4.6 collective-permute-start.52
  452.5 10.0 collective-permute-start.24
  462.5 12.5 %shard_map.53 = (f32[6,512,256]{2,1,0:T(8,128)}, f32[5,512,256]{2,1,0:T(8,128)}, f32[6,512,256]{2,1,0:T(8,128)}) custom-call(s32[98]{0:T(128)} %pad_add_fusion.8.s, f32[2048,4096]{1,0:T(8,128)} %h_ref.17, f32[4,512,512]{2,1,0:T(8,128)} %bitcast.65, bf16[8,512,512]{2,1,0:T(8,128)(2,1)} %get-tuple-element.49.ch, bf16[8,512,512]{2,1,0:T(8,128)(2,1)} %get-tuple-element.50.cl), custom_call_target="tpu_custom_call" | custom-call | flops 9663676416 | bytes 18874368 | tf_op jit(solution)/shard_map/pallas_call | solution.py:175
  477.0 94.7 %collective-permute-done.24 = f32[2,256,256]{2,1,0:T(8,128)S(1)} collective-permute-done((f32[2,256,256]{2,1,0:T(8,128)S(1)}, f32[2,256,256]{2,1,0:T(8,128)S(1)}, u32[]{:S(2)}, u32[]{:S(2)}) %collective-permute-start.24) | collective-permute-done | bytes 524320 | tf_op jit(solution)/shard_map/ppermute | solution.py:74
  576.4 80.5 %collective-permute-done.32.b_ref = f32[4,512,256]{2,1,0:T(8,128)S(1)} collective-permute-done((f32[4,512,256]{2,1,0:T(8,128)}, f32[4,512,256]{2,1,0:T(8,128)S(1)}, u32[]{:S(2)}, u32[]{:S(2)}) %collective-permute-start.32) | collective-permute-done | bytes 2097184 | tf_op jit(solution)/shard_map/ppermute | solution.py:74
  658.8 8.4 shard_map.52
  668.8 11.2 %collective-permute-start.34 = (f32[4,256,256]{2,1,0:T(8,128)}, f32[4,256,256]{2,1,0:T(8,128)S(1)}, u32[]{:S(2)}, u32[]{:S(2)}) collective-permute-start(f32[4,256,256]{2,1,0:T(8,128)} %get-tuple-element.65), channel_id=1, source_target_pairs={{0,1},{1,2},{2,3},{4,5},{5,6},{6,7},{8,9},{9,10},{10,11},{12,13},{... | collective-permute-start | bytes 3145736 | tf_op jit(solution)/shard_map/ppermute | solution.py:74
  680.1 11.7 %shard_map.54 = (f32[6,256,256]{2,1,0:T(8,128)}, f32[6,256,256]{2,1,0:T(8,128)}, f32[5,256,256]{2,1,0:T(8,128)}, f32[5,256,256]{2,1,0:T(8,128)}, f32[6,256,256]{2,1,0:T(8,128)}, /*index=5*/f32[6,256,256]{2,1,0:T(8,128)}) custom-call(s32[98]{0:T(128)} %pad_add_fusion.8.s, f32[6,512,256]{2,1,0:T(8,128)} %get-tuple-element.71.r_ref, ...), custom_call_target="tpu_custom_call" | custom-call | flops 4831838208 | bytes 18874368 | tf_op jit(solution)/shard_map/pallas_call | solution.py:235
  696.2 15.2 %shard_map.56 = (f32[8,256,256]{2,1,0:T(8,128)}, f32[8,256,256]{2,1,0:T(8,128)}, f32[7,256,256]{2,1,0:T(8,128)}, f32[7,256,256]{2,1,0:T(8,128)}, f32[8,256,256]{2,1,0:T(8,128)}, /*index=5*/f32[8,256,256]{2,1,0:T(8,128)}) custom-call(s32[98]{0:T(128)} %pad_add_fusion.8.s, f32[8,512,256]{2,1,0:T(8,128)} %get-tuple-element.80.r_ref, ...), custom_call_target="tpu_custom_call" | custom-call | flops 6442450944 | bytes 25165824 | tf_op jit(solution)/shard_map/pallas_call | solution.py:235
  713.0 6.1 collective-permute-start.54
  719.1 7.3 collective-permute-done.38
  726.4 4.3 collective-permute-start.58
  731.5 76.8 %collective-permute-start.44 = (f32[6,256,256]{2,1,0:T(8,128)}, f32[6,256,256]{2,1,0:T(8,128)S(1)}, u32[]{:S(2)}, u32[]{:S(2)}) collective-permute-start(f32[6,256,256]{2,1,0:T(8,128)} %get-tuple-element.74), channel_id=1, source_target_pairs={{0,1},{1,2},{2,3},{4,5},{5,6},{6,7},{8,9},{9,10},{10,11},{12,13},{... | collective-permute-start | bytes 4718600 | tf_op jit(solution)/shard_map/ppermute | solution.py:74
  810.2 4.2 collective-permute-start.51
  816.1 33.9 %collective-permute-done.44 = f32[6,256,256]{2,1,0:T(8,128)S(1)} collective-permute-done((f32[6,256,256]{2,1,0:T(8,128)}, f32[6,256,256]{2,1,0:T(8,128)S(1)}, u32[]{:S(2)}, u32[]{:S(2)}) %collective-permute-start.44) | collective-permute-done | bytes 1572896 | tf_op jit(solution)/shard_map/ppermute | solution.py:74
  854.6 24.3 %collective-permute-done.48 = f32[6,256,256]{2,1,0:T(8,128)S(1)} collective-permute-done((f32[6,256,256]{2,1,0:T(8,128)}, f32[6,256,256]{2,1,0:T(8,128)S(1)}, u32[]{:S(2)}, u32[]{:S(2)}) %collective-permute-start.48) | collective-permute-done | bytes 1572896 | tf_op jit(solution)/shard_map/ppermute | solution.py:74
  878.9 11.4 %collective-permute-start.60 = (f32[8,256,256]{2,1,0:T(8,128)}, f32[8,256,256]{2,1,0:T(8,128)}, u32[]{:S(2)}, u32[]{:S(2)}) collective-permute-start(f32[8,256,256]{2,1,0:T(8,128)} %pad_add_fusion.lt), channel_id=1, source_target_pairs={{0,28},{4,0},{8,4},{12,8},{16,12},{20,16},{24,20},{28,24},{1,29},{... | collective-permute-start | bytes 6291464 | tf_op jit(solution)/shard_map/ppermute | solution.py:68
  892.9 13.9 %shard_map.57.rest_6_ = f32[2048,4096]{1,0:T(8,128)} custom-call(s32[24]{0:T(128)} %constant.91.s, f32[2048,4096]{1,0:T(8,128)} %h_ref.17), custom_call_target="tpu_custom_call" | custom-call | flops 3145728 | bytes 25165824 | tf_op jit(solution)/shard_map/pallas_call | solution.py:128
  906.8 8.1 shard_map.46
  925.7 34.7 %collective-permute-done.50.rest_4_.rest_0_ = f32[6,256,256]{2,1,0:T(8,128)} collective-permute-done((f32[6,256,256]{2,1,0:T(8,128)}, f32[6,256,256]{2,1,0:T(8,128)}, u32[]{:S(2)}, u32[]{:S(2)}) %collective-permute-start.50) | collective-permute-done | bytes 1572896 | tf_op jit(solution)/shard_map/ppermute | solution.py:68
  964.7 25.5 %shard_map.58.rest_8_ = f32[2048,4096]{1,0:T(8,128)} custom-call(s32[98]{0:T(128)} %pad_add_fusion.8.s, f32[2048,4096]{1,0:T(8,128)} %h_ref.17, f32[4,512,512]{2,1,0:T(8,128)} %bitcast.54, f32[4,512,256]{2,1,0:T(8,128)} %copy-done, f32[4,512,512]{2,1,0:T(8,128)} %bitcast.58, ...), custom_call_target="tpu_custom_call", output_to_operand_aliasing={{}: (17, {})} | custom-call | flops 19327352832 | bytes 50331648 | tf_op jit(solution)/shard_map/pallas_call | solution.py:379
  990.3 3.7 collective-permute-start.31
  994.0 17.5 %collective-permute-done.40.rest_4_.rest_0_ = f32[4,256,256]{2,1,0:T(8,128)} collective-permute-done((f32[4,256,256]{2,1,0:T(8,128)}, f32[4,256,256]{2,1,0:T(8,128)}, u32[]{:S(2)}, u32[]{:S(2)}) %collective-permute-start.40) | collective-permute-done | bytes 1048608 | tf_op jit(solution)/shard_map/ppermute | solution.py:68
  1016.5 11.8 %collective-permute-done.46.rest_2_.rest_6_ = f32[6,256,256]{2,1,0:T(8,128)} collective-permute-done((f32[6,256,256]{2,1,0:T(8,128)}, f32[6,256,256]{2,1,0:T(8,128)}, u32[]{:S(2)}, u32[]{:S(2)}) %collective-permute-start.46) | collective-permute-done | bytes 1572896 | tf_op jit(solution)/shard_map/ppermute | solution.py:68
  1028.4 17.1 %shard_map.59.rest_8_ = f32[2048,4096]{1,0:T(8,128)} custom-call(s32[98]{0:T(128)} %pad_add_fusion.8.s, f32[2048,4096]{1,0:T(8,128)} %h_ref.17, f32[4,512,512]{2,1,0:T(8,128)} %bitcast.55, f32[4,512,256]{2,1,0:T(8,128)} %copy-done, f32[4,512,512]{2,1,0:T(8,128)} %bitcast.59, ...), custom_call_target="tpu_custom_call", output_to_operand_aliasing={{}: (19, {})} | custom-call | flops 14495514624 | bytes 37748736 | tf_op jit(solution)/shard_map/pallas_call | solution.py:379
  1045.5 5.3 collective-permute-start.30
  1050.8 5.6 collective-permute-done.36.rest_2_.rest_4_
  1057.3 11.7 %shard_map.60.rest_6_ = f32[2048,4096]{1,0:T(8,128)} custom-call(s32[98]{0:T(128)} %pad_add_fusion.8.s, f32[2048,4096]{1,0:T(8,128)} %h_ref.17, f32[4,512,512]{2,1,0:T(8,128)} %bitcast.56, f32[4,512,256]{2,1,0:T(8,128)} %copy-done, f32[4,512,512]{2,1,0:T(8,128)} %bitcast.60, ...), custom_call_target="tpu_custom_call", output_to_operand_aliasing={{}: (19, {})} | custom-call | flops 9663676416 | bytes 25165824 | tf_op jit(solution)/shard_map/pallas_call | solution.py:379
  1069.9 9.2 shard_map.61
  (164 shorter events, 102.0 us)
Async XLA Ops:
  6.5 84.0 %all-gather.11.cloned.1.call-start = ((), (), s32[]{:S(2)}) async-start(), calls=%async_computation.2 | async-start | bytes 5242880 | tf_op jit(solution)/shard_map/all_gather | solution.py:417
  10.2 161.2 %all-gather.7.cloned.1.call-start = ((), (), s32[]{:S(2)}) async-start(), calls=%async_computation | async-start | bytes 5242880 | tf_op jit(solution)/shard_map/all_gather | solution.py:417
  10.9 241.3 %all-gather.9.cloned.1.call-start = ((), (), s32[]{:S(2)}) async-start(), calls=%async_computation.1 | async-start | bytes 5242880 | tf_op jit(solution)/shard_map/all_gather | solution.py:417
  94.2 82.4 %collective-permute-start.8 = (f32[4,128,512]{2,1,0:T(8,128)}, f32[4,128,512]{2,1,0:T(8,128)S(1)}, u32[]{:S(2)}, u32[]{:S(2)}) collective-permute-start(f32[4,128,512]{2,1,0:T(8,128)} %get-tuple-element.92), channel_id=1, source_target_pairs={{0,4},{5,9},{10,14},{15,3},{16,20},{21,25},{26,30},{31,19}} | collective-permute-start | bytes 3145736 | tf_op jit(solution)/shard_map/ppermute | solution.py:424
  94.9 83.0 %collective-permute-start.10 = (f32[4,128,512]{2,1,0:T(8,128)}, f32[4,128,512]{2,1,0:T(8,128)}, u32[]{:S(2)}, u32[]{:S(2)}) collective-permute-start(f32[4,128,512]{2,1,0:T(8,128)} %get-tuple-element.93), channel_id=1, source_target_pairs={{0,12},{5,1},{10,6},{15,11},{16,28},{21,17},{26,22},{31,27}} | collective-permute-start | bytes 3145736 | tf_op jit(solution)/shard_map/ppermute | solution.py:424
  96.6 81.3 %collective-permute-start.9 = (f32[4,128,512]{2,1,0:T(8,128)}, f32[4,128,512]{2,1,0:T(8,128)}, u32[]{:S(2)}, u32[]{:S(2)}) collective-permute-start(f32[4,128,512]{2,1,0:T(8,128)} %get-tuple-element.94), channel_id=1, source_target_pairs={{0,8},{5,13},{10,2},{15,7},{16,24},{21,29},{26,18},{31,23}} | collective-permute-start | bytes 3145736 | tf_op jit(solution)/shard_map/ppermute | solution.py:424
  175.8 78.9 %collective-permute-start.19 = (f32[4,128,512]{2,1,0:T(8,128)}, f32[4,128,512]{2,1,0:T(8,128)S(1)}, u32[]{:S(2)}, u32[]{:S(2)}) collective-permute-start(f32[4,128,512]{2,1,0:T(8,128)} %get-tuple-element.90), channel_id=1, source_target_pairs={{0,12},{5,1},{10,6},{15,11},{16,28},{21,17},{26,22},{31,27}} | collective-permute-start | bytes 3145736 | tf_op jit(solution)/shard_map/ppermute | solution.py:424
  176.6 78.8 %collective-permute-start.18 = (f32[4,128,512]{2,1,0:T(8,128)}, f32[4,128,512]{2,1,0:T(8,128)}, u32[]{:S(2)}, u32[]{:S(2)}) collective-permute-start(f32[4,128,512]{2,1,0:T(8,128)} %get-tuple-element.91), channel_id=1, source_target_pairs={{0,8},{5,13},{10,2},{15,7},{16,24},{21,29},{26,18},{31,23}} | collective-permute-start | bytes 3145736 | tf_op jit(solution)/shard_map/ppermute | solution.py:424
  180.7 75.4 %collective-permute-start.13 = (f32[4,128,512]{2,1,0:T(8,128)S(1)}, f32[4,128,512]{2,1,0:T(8,128)}, u32[]{:S(2)}, u32[]{:S(2)}) collective-permute-start(f32[4,128,512]{2,1,0:T(8,128)S(1)} %fusion.3), channel_id=1, source_target_pairs={{0,24},{4,28},{8,16},{12,20},{16,8},{20,12},{24,0},{28,4},{1,25},{... | collective-permute-start | bytes 3145736 | tf_op jit(solution)/shard_map/ppermute | solution.py:84
  184.9 74.6 %collective-permute-start.12 = (f32[4,128,512]{2,1,0:T(8,128)S(1)}, f32[4,128,512]{2,1,0:T(8,128)}, u32[]{:S(2)}, u32[]{:S(2)}) collective-permute-start(f32[4,128,512]{2,1,0:T(8,128)S(1)} %fusion.3), channel_id=1, source_target_pairs={{0,16},{4,20},{8,24},{12,28},{16,0},{20,4},{24,8},{28,12},{1,17},{... | collective-permute-start | bytes 3145736 | tf_op jit(solution)/shard_map/ppermute | solution.py:84
  186.4 76.2 %collective-permute-start.11 = (f32[4,128,512]{2,1,0:T(8,128)S(1)}, f32[4,128,512]{2,1,0:T(8,128)}, u32[]{:S(2)}, u32[]{:S(2)}) collective-permute-start(f32[4,128,512]{2,1,0:T(8,128)S(1)} %fusion.3), channel_id=1, source_target_pairs={{0,8},{4,12},{8,0},{12,4},{16,24},{20,28},{24,16},{28,20},{1,9},{5... | collective-permute-start | bytes 3145736 | tf_op jit(solution)/shard_map/ppermute | solution.py:84
  256.2 47.9 %collective-permute-start.2 = (f32[4,128,512]{2,1,0:T(8,128)S(1)}, f32[4,128,512]{2,1,0:T(8,128)S(1)}, u32[]{:S(2)}, u32[]{:S(2)}) collective-permute-start(f32[4,128,512]{2,1,0:T(8,128)S(1)} %get-tuple-element.97), channel_id=1, source_target_pairs={{0,8},{5,13},{10,2},{15,7},{16,24},{21,29},{26,18},{31,23}} | collective-permute-start | bytes 3145736 | tf_op jit(solution)/shard_map/ppermute | solution.py:424
  259.5 66.5 %collective-permute-start.22 = (f32[4,128,512]{2,1,0:T(8,128)S(1)}, f32[4,128,512]{2,1,0:T(8,128)S(1)}, u32[]{:S(2)}, u32[]{:S(2)}) collective-permute-start(f32[4,128,512]{2,1,0:T(8,128)S(1)} %fusion.1), channel_id=1, source_target_pairs={{0,24},{4,28},{8,16},{12,20},{16,8},{20,12},{24,0},{28,4},{1,25},{... | collective-permute-start | bytes 3145736 | tf_op jit(solution)/shard_map/ppermute | solution.py:84
  262.7 65.4 %collective-permute-start.21 = (f32[4,128,512]{2,1,0:T(8,128)S(1)}, f32[4,128,512]{2,1,0:T(8,128)S(1)}, u32[]{:S(2)}, u32[]{:S(2)}) collective-permute-start(f32[4,128,512]{2,1,0:T(8,128)S(1)} %fusion.1), channel_id=1, source_target_pairs={{0,16},{4,20},{8,24},{12,28},{16,0},{20,4},{24,8},{28,12},{1,17},{... | collective-permute-start | bytes 3145736 | tf_op jit(solution)/shard_map/ppermute | solution.py:84
  268.6 111.4 %collective-permute-start.14 = (f32[4,4,128,512]{3,2,1,0:T(8,128)}, f32[4,4,128,512]{3,2,1,0:T(8,128)}, u32[]{:S(2)}, u32[]{:S(2)}) collective-permute-start(f32[4,4,128,512]{3,2,1,0:T(8,128)} %pad_maximum_fusion.1.same_ref), channel_id=1, source_target_pairs={{0,4},{4,0},{8,12},{12,8},{16,20},{20,16},{24,28},{28,24},{1,5},{5... | collective-permute-start | bytes 12582920 | tf_op jit(solution)/shard_map/ppermute | solution.py:84
  268.6 80.4 %collective-permute-start.20 = (f32[4,128,512]{2,1,0:T(8,128)S(1)}, f32[4,128,512]{2,1,0:T(8,128)S(1)}, u32[]{:S(2)}, u32[]{:S(2)}) collective-permute-start(f32[4,128,512]{2,1,0:T(8,128)S(1)} %fusion.1), channel_id=1, source_target_pairs={{0,8},{4,12},{8,0},{12,4},{16,24},{20,28},{24,16},{28,20},{1,9},{5... | collective-permute-start | bytes 3145736 | tf_op jit(solution)/shard_map/ppermute | solution.py:84
  305.8 56.0 %collective-permute-start.6 = (f32[4,128,512]{2,1,0:T(8,128)S(1)}, f32[4,128,512]{2,1,0:T(8,128)S(1)}, u32[]{:S(2)}, u32[]{:S(2)}) collective-permute-start(f32[4,128,512]{2,1,0:T(8,128)S(1)} %fusion.5), channel_id=1, source_target_pairs={{0,24},{4,28},{8,16},{12,20},{16,8},{20,12},{24,0},{28,4},{1,25},{... | collective-permute-start | bytes 3145736 | tf_op jit(solution)/shard_map/ppermute | solution.py:84
  328.1 44.9 %collective-permute-start.4 = (f32[4,128,512]{2,1,0:T(8,128)S(1)}, f32[4,128,512]{2,1,0:T(8,128)S(1)}, u32[]{:S(2)}, u32[]{:S(2)}) collective-permute-start(f32[4,128,512]{2,1,0:T(8,128)S(1)} %fusion.5), channel_id=1, source_target_pairs={{0,8},{4,12},{8,0},{12,4},{16,24},{20,28},{24,16},{28,20},{1,9},{5... | collective-permute-start | bytes 3145736 | tf_op jit(solution)/shard_map/ppermute | solution.py:84
  351.7 64.7 %collective-permute-start.23 = (f32[4,4,128,512]{3,2,1,0:T(8,128)}, f32[4,4,128,512]{3,2,1,0:T(8,128)}, u32[]{:S(2)}, u32[]{:S(2)}) collective-permute-start(f32[4,4,128,512]{3,2,1,0:T(8,128)} %pad_maximum_fusion.2.same_ref), channel_id=1, source_target_pairs={{0,4},{4,0},{8,12},{12,8},{16,20},{20,16},{24,28},{28,24},{1,5},{5... | collective-permute-start | bytes 12582920 | tf_op jit(solution)/shard_map/ppermute | solution.py:84
  375.8 75.3 %collective-permute-start.7 = (f32[4,4,128,512]{3,2,1,0:T(8,128)}, f32[4,4,128,512]{3,2,1,0:T(8,128)}, u32[]{:S(2)}, u32[]{:S(2)}) collective-permute-start(f32[4,4,128,512]{3,2,1,0:T(8,128)} %pad_maximum_fusion.same_ref), channel_id=1, source_target_pairs={{0,4},{4,0},{8,12},{12,8},{16,20},{20,16},{24,28},{28,24},{1,5},{5... | collective-permute-start | bytes 12582920 | tf_op jit(solution)/shard_map/ppermute | solution.py:84
  379.5 66.9 %collective-permute-start = (f32[4,512,256]{2,1,0:T(8,128)}, f32[4,512,256]{2,1,0:T(8,128)S(1)}, u32[]{:S(2)}, u32[]{:S(2)}) collective-permute-start(f32[4,512,256]{2,1,0:T(8,128)} %slice.16), channel_id=1, source_target_pairs={{0,4},{4,8},{8,12},{12,16},{16,20},{20,24},{24,28},{28,0},{1,5},{5... | collective-permute-start | bytes 6291464 | tf_op jit(solution)/shard_map/ppermute | solution.py:68
  442.2 131.6 %collective-permute-start.33 = (f32[3,512,256]{2,1,0:T(8,128)}, f32[3,512,256]{2,1,0:T(8,128)}, u32[]{:S(2)}, u32[]{:S(2)}) collective-permute-start(f32[3,512,256]{2,1,0:T(8,128)} %get-tuple-element.64), channel_id=1, source_target_pairs={{0,3},{4,7},{8,11},{12,15},{16,19},{20,23},{24,27},{28,31}} | collective-permute-start | bytes 4718600 | tf_op jit(solution)/shard_map/ppermute | solution.py:79
  444.0 249.3 %collective-permute-start.53 = (f32[7,512,256]{2,1,0:T(8,128)}, f32[7,512,256]{2,1,0:T(8,128)}, u32[]{:S(2)}, u32[]{:S(2)}) collective-permute-start(f32[7,512,256]{2,1,0:T(8,128)} %get-tuple-element.82), channel_id=1, source_target_pairs={{0,3},{4,7},{8,11},{12,15},{16,19},{20,23},{24,27},{28,31}} | collective-permute-start | bytes 11010056 | tf_op jit(solution)/shard_map/ppermute | solution.py:79
  446.5 249.0 %collective-permute-start.52 = (f32[8,512,256]{2,1,0:T(8,128)}, f32[8,512,256]{2,1,0:T(8,128)}, u32[]{:S(2)}, u32[]{:S(2)}) collective-permute-start(f32[8,512,256]{2,1,0:T(8,128)} %get-tuple-element.81), channel_id=1, source_target_pairs={{1,0},{2,1},{3,2},{5,4},{6,5},{7,6},{9,8},{10,9},{11,10},{13,12},{... | collective-permute-start | bytes 12582920 | tf_op jit(solution)/shard_map/ppermute | solution.py:74
  452.5 119.2 %collective-permute-start.24 = (f32[2,256,256]{2,1,0:T(8,128)S(1)}, f32[2,256,256]{2,1,0:T(8,128)S(1)}, u32[]{:S(2)}, u32[]{:S(2)}) collective-permute-start(f32[2,256,256]{2,1,0:T(8,128)S(1)} %copy-done.20), channel_id=1, source_target_pairs={{0,1},{1,2},{2,3},{4,5},{5,6},{6,7},{8,9},{9,10},{10,11},{12,13},{... | collective-permute-start | bytes 1572872 | tf_op jit(solution)/shard_map/ppermute | solution.py:74
  475.0 193.8 %collective-permute-start.42 = (f32[6,512,256]{2,1,0:T(8,128)}, f32[6,512,256]{2,1,0:T(8,128)}, u32[]{:S(2)}, u32[]{:S(2)}) collective-permute-start(f32[6,512,256]{2,1,0:T(8,128)} %get-tuple-element.72), channel_id=1, source_target_pairs={{1,0},{2,1},{3,2},{5,4},{6,5},{7,6},{9,8},{10,9},{11,10},{13,12},{... | collective-permute-start | bytes 9437192 | tf_op jit(solution)/shard_map/ppermute | solution.py:74
  571.7 95.6 %collective-permute-start.43 = (f32[5,512,256]{2,1,0:T(8,128)}, f32[5,512,256]{2,1,0:T(8,128)}, u32[]{:S(2)}, u32[]{:S(2)}) collective-permute-start(f32[5,512,256]{2,1,0:T(8,128)} %get-tuple-element.73), channel_id=1, source_target_pairs={{0,3},{4,7},{8,11},{12,15},{16,19},{20,23},{24,27},{28,31}} | collective-permute-start | bytes 7864328 | tf_op jit(solution)/shard_map/ppermute | solution.py:79
  573.8 83.1 %collective-permute-start.32 = (f32[4,512,256]{2,1,0:T(8,128)}, f32[4,512,256]{2,1,0:T(8,128)S(1)}, u32[]{:S(2)}, u32[]{:S(2)}) collective-permute-start(f32[4,512,256]{2,1,0:T(8,128)} %get-tuple-element.63), channel_id=1, source_target_pairs={{1,0},{2,1},{3,2},{5,4},{6,5},{7,6},{9,8},{10,9},{11,10},{13,12},{... | collective-permute-start | bytes 6291464 | tf_op jit(solution)/shard_map/ppermute | solution.py:74
  667.3 44.2 %collective-permute-start.35 = (f32[3,256,256]{2,1,0:T(8,128)}, f32[3,256,256]{2,1,0:T(8,128)}, u32[]{:S(2)}, u32[]{:S(2)}) collective-permute-start(f32[3,256,256]{2,1,0:T(8,128)} %get-tuple-element.66), channel_id=1, source_target_pairs={{3,0},{7,4},{11,8},{15,12},{19,16},{23,20},{27,24},{31,28}} | collective-permute-start | bytes 2359304 | tf_op jit(solution)/shard_map/ppermute | solution.py:79
  668.8 44.2 %collective-permute-start.34 = (f32[4,256,256]{2,1,0:T(8,128)}, f32[4,256,256]{2,1,0:T(8,128)S(1)}, u32[]{:S(2)}, u32[]{:S(2)}) collective-permute-start(f32[4,256,256]{2,1,0:T(8,128)} %get-tuple-element.65), channel_id=1, source_target_pairs={{0,1},{1,2},{2,3},{4,5},{5,6},{6,7},{8,9},{9,10},{10,11},{12,13},{... | collective-permute-start | bytes 3145736 | tf_op jit(solution)/shard_map/ppermute | solution.py:74
  711.4 96.8 %collective-permute-start.55 = (f32[7,256,256]{2,1,0:T(8,128)}, f32[7,256,256]{2,1,0:T(8,128)S(1)}, u32[]{:S(2)}, u32[]{:S(2)}) collective-permute-start(f32[7,256,256]{2,1,0:T(8,128)} %get-tuple-element.84), channel_id=1, source_target_pairs={{3,0},{7,4},{11,8},{15,12},{19,16},{23,20},{27,24},{31,28}} | collective-permute-start | bytes 5505032 | tf_op jit(solution)/shard_map/ppermute | solution.py:79
  713.0 97.2 %collective-permute-start.54 = (f32[8,256,256]{2,1,0:T(8,128)}, f32[8,256,256]{2,1,0:T(8,128)S(1)}, u32[]{:S(2)}, u32[]{:S(2)}) collective-permute-start(f32[8,256,256]{2,1,0:T(8,128)} %get-tuple-element.83), channel_id=1, source_target_pairs={{0,1},{1,2},{2,3},{4,5},{5,6},{6,7},{8,9},{9,10},{10,11},{12,13},{... | collective-permute-start | bytes 6291464 | tf_op jit(solution)/shard_map/ppermute | solution.py:74
  726.4 126.2 %collective-permute-start.58 = (f32[8,256,256]{2,1,0:T(8,128)}, f32[8,256,256]{2,1,0:T(8,128)S(1)}, u32[]{:S(2)}, u32[]{:S(2)}) collective-permute-start(f32[8,256,256]{2,1,0:T(8,128)} %get-tuple-element.86), channel_id=1, source_target_pairs={{0,1},{1,2},{2,3},{4,5},{5,6},{6,7},{8,9},{9,10},{10,11},{12,13},{... | collective-permute-start | bytes 6291464 | tf_op jit(solution)/shard_map/ppermute | solution.py:74
  730.7 119.3 %collective-permute-start.59 = (f32[7,256,256]{2,1,0:T(8,128)}, f32[7,256,256]{2,1,0:T(8,128)S(1)}, u32[]{:S(2)}, u32[]{:S(2)}) collective-permute-start(f32[7,256,256]{2,1,0:T(8,128)} %get-tuple-element.87), channel_id=1, source_target_pairs={{3,0},{7,4},{11,8},{15,12},{19,16},{23,20},{27,24},{31,28}} | collective-permute-start | bytes 5505032 | tf_op jit(solution)/shard_map/ppermute | solution.py:79
  731.5 118.5 %collective-permute-start.44 = (f32[6,256,256]{2,1,0:T(8,128)}, f32[6,256,256]{2,1,0:T(8,128)S(1)}, u32[]{:S(2)}, u32[]{:S(2)}) collective-permute-start(f32[6,256,256]{2,1,0:T(8,128)} %get-tuple-element.74), channel_id=1, source_target_pairs={{0,1},{1,2},{2,3},{4,5},{5,6},{6,7},{8,9},{9,10},{10,11},{12,13},{... | collective-permute-start | bytes 4718600 | tf_op jit(solution)/shard_map/ppermute | solution.py:74
  808.3 70.7 %collective-permute-start.48 = (f32[6,256,256]{2,1,0:T(8,128)}, f32[6,256,256]{2,1,0:T(8,128)S(1)}, u32[]{:S(2)}, u32[]{:S(2)}) collective-permute-start(f32[6,256,256]{2,1,0:T(8,128)} %get-tuple-element.77), channel_id=1, source_target_pairs={{0,1},{1,2},{2,3},{4,5},{5,6},{6,7},{8,9},{9,10},{10,11},{12,13},{... | collective-permute-start | bytes 4718600 | tf_op jit(solution)/shard_map/ppermute | solution.py:74
  810.2 81.5 %collective-permute-start.51 = (f32[6,256,256]{2,1,0:T(8,128)}, f32[6,256,256]{2,1,0:T(8,128)}, u32[]{:S(2)}, u32[]{:S(2)}) collective-permute-start(f32[6,256,256]{2,1,0:T(8,128)} %get-tuple-element.79.rt), channel_id=1, source_target_pairs={{0,28},{4,0},{8,4},{12,8},{16,12},{20,16},{24,20},{28,24},{1,29},{... | collective-permute-start | bytes 4718600 | tf_op jit(solution)/shard_map/ppermute | solution.py:68
  850.0 75.0 %collective-permute-start.57 = (f32[8,256,256]{2,1,0:T(8,128)}, f32[8,256,256]{2,1,0:T(8,128)S(1)}, u32[]{:S(2)}, u32[]{:S(2)}) collective-permute-start(f32[8,256,256]{2,1,0:T(8,128)} %get-tuple-element.85.rb), channel_id=1, source_target_pairs={{0,4},{4,8},{8,12},{12,16},{16,20},{20,24},{24,28},{28,0},{1,5},{5... | collective-permute-start | bytes 6291464 | tf_op jit(solution)/shard_map/ppermute | solution.py:68
  850.0 75.4 %collective-permute-start.61 = (f32[8,256,256]{2,1,0:T(8,128)}, f32[8,256,256]{2,1,0:T(8,128)}, u32[]{:S(2)}, u32[]{:S(2)}) collective-permute-start(f32[8,256,256]{2,1,0:T(8,128)} %get-tuple-element.88.rt), channel_id=1, source_target_pairs={{0,28},{4,0},{8,4},{12,8},{16,12},{20,16},{24,20},{28,24},{1,29},{... | collective-permute-start | bytes 6291464 | tf_op jit(solution)/shard_map/ppermute | solution.py:68
  852.7 110.5 %collective-permute-start.56 = (f32[8,256,256]{2,1,0:T(8,128)}, f32[8,256,256]{2,1,0:T(8,128)}, u32[]{:S(2)}, u32[]{:S(2)}) collective-permute-start(f32[8,256,256]{2,1,0:T(8,128)} %pad_add_fusion.1.lb), channel_id=1, source_target_pairs={{0,4},{4,8},{8,12},{12,16},{16,20},{20,24},{24,28},{28,0},{1,5},{5... | collective-permute-start | bytes 6291464 | tf_op jit(solution)/shard_map/ppermute | solution.py:68
  878.9 84.3 %collective-permute-start.60 = (f32[8,256,256]{2,1,0:T(8,128)}, f32[8,256,256]{2,1,0:T(8,128)}, u32[]{:S(2)}, u32[]{:S(2)}) collective-permute-start(f32[8,256,256]{2,1,0:T(8,128)} %pad_add_fusion.lt), channel_id=1, source_target_pairs={{0,28},{4,0},{8,4},{12,8},{16,12},{20,16},{24,20},{28,24},{1,29},{... | collective-permute-start | bytes 6291464 | tf_op jit(solution)/shard_map/ppermute | solution.py:68
  891.8 68.6 %collective-permute-start.50 = (f32[6,256,256]{2,1,0:T(8,128)}, f32[6,256,256]{2,1,0:T(8,128)}, u32[]{:S(2)}, u32[]{:S(2)}) collective-permute-start(f32[6,256,256]{2,1,0:T(8,128)} %pad_add_fusion.2.lt), channel_id=1, source_target_pairs={{0,28},{4,0},{8,4},{12,8},{16,12},{20,16},{24,20},{28,24},{1,29},{... | collective-permute-start | bytes 4718600 | tf_op jit(solution)/shard_map/ppermute | solution.py:68
  925.0 120.5 %collective-permute-start.29 = (f32[2,256,256]{2,1,0:T(8,128)}, f32[2,256,256]{2,1,0:T(8,128)}, u32[]{:S(2)}, u32[]{:S(2)}) collective-permute-start(f32[2,256,256]{2,1,0:T(8,128)} %get-tuple-element.60.rt), channel_id=1, source_target_pairs={{0,28},{4,0},{8,4},{12,8},{16,12},{20,16},{24,20},{28,24},{1,29},{... | collective-permute-start | bytes 1572872 | tf_op jit(solution)/shard_map/ppermute | solution.py:68
  925.4 64.8 %collective-permute-start.41 = (f32[4,256,256]{2,1,0:T(8,128)}, f32[4,256,256]{2,1,0:T(8,128)S(1)}, u32[]{:S(2)}, u32[]{:S(2)}) collective-permute-start(f32[4,256,256]{2,1,0:T(8,128)} %get-tuple-element.70.rt), channel_id=1, source_target_pairs={{0,28},{4,0},{8,4},{12,8},{16,12},{20,16},{24,20},{28,24},{1,29},{... | collective-permute-start | bytes 3145736 | tf_op jit(solution)/shard_map/ppermute | solution.py:68
  960.4 51.1 %collective-permute-start.40 = (f32[4,256,256]{2,1,0:T(8,128)}, f32[4,256,256]{2,1,0:T(8,128)}, u32[]{:S(2)}, u32[]{:S(2)}) collective-permute-start(f32[4,256,256]{2,1,0:T(8,128)} %pad_add_fusion.4.lt), channel_id=1, source_target_pairs={{0,28},{4,0},{8,4},{12,8},{16,12},{20,16},{24,20},{28,24},{1,29},{... | collective-permute-start | bytes 3145736 | tf_op jit(solution)/shard_map/ppermute | solution.py:68
  963.2 51.1 %collective-permute-start.47 = (f32[6,256,256]{2,1,0:T(8,128)}, f32[6,256,256]{2,1,0:T(8,128)}, u32[]{:S(2)}, u32[]{:S(2)}) collective-permute-start(f32[6,256,256]{2,1,0:T(8,128)} %get-tuple-element.76.rb), channel_id=1, source_target_pairs={{0,4},{4,8},{8,12},{12,16},{16,20},{20,24},{24,28},{28,0},{1,5},{5... | collective-permute-start | bytes 4718600 | tf_op jit(solution)/shard_map/ppermute | solution.py:68
  963.2 65.2 %collective-permute-start.46 = (f32[6,256,256]{2,1,0:T(8,128)}, f32[6,256,256]{2,1,0:T(8,128)}, u32[]{:S(2)}, u32[]{:S(2)}) collective-permute-start(f32[6,256,256]{2,1,0:T(8,128)} %pad_add_fusion.3.lb), channel_id=1, source_target_pairs={{0,4},{4,8},{8,12},{12,16},{16,20},{20,24},{24,28},{28,0},{1,5},{5... | collective-permute-start | bytes 4718600 | tf_op jit(solution)/shard_map/ppermute | solution.py:68
  990.3 78.8 %collective-permute-start.31 = (f32[2,256,256]{2,1,0:T(8,128)}, f32[2,256,256]{2,1,0:T(8,128)}, u32[]{:S(2)}, u32[]{:S(2)}) collective-permute-start(f32[2,256,256]{2,1,0:T(8,128)} %get-tuple-element.61.rb), channel_id=1, source_target_pairs={{0,4},{4,8},{8,12},{12,16},{16,20},{20,24},{24,28},{28,0},{1,5},{5... | collective-permute-start | bytes 1572872 | tf_op jit(solution)/shard_map/ppermute | solution.py:68
  (38 other events, 1214.4 us)
Sparse Core Ops, SparseCore 0:
  10.3 80.2 all-gather.10
  92.1 79.2 all-gather.6
  173.0 79.2 all-gather.8

commit v2 on v1

--- a/solution.py
+++ b/solution.py
@@ -140,7 +140,7 @@
 
         @pl.when(i == 0)
         def _():
-            qh[...], ql[...] = split(q_ref[0].T)
+            qh[...], ql[...] = split(q_ref[0, 0].T)
 
         do_left = upper & flag(s, g, 0, r)
         do_right = upper & flag(s, g, 0, c)
@@ -177,7 +177,7 @@
         n,
         [
             pl.BlockSpec((W, W), lambda i, s: (k, lo_m + i)),
-            pl.BlockSpec((1, W, W), lambda i, s: (k, 0, 0)),
+            pl.BlockSpec((1, 1, W, W), lambda i, s: (0, k, 0, 0)),
             pl.BlockSpec((1, W, W), lambda i, s: (lo_m + i, 0, 0)),
             pl.BlockSpec((1, W, W), lambda i, s: (lo_m + i, 0, 0)),
         ],
@@ -255,7 +255,7 @@
 
 def finish(g, k, scalars, matrix, factors, col_hi, col_lo, own, below, above, out):
     W, half, lo_m, n = g.win, g.half, g.first(k), g.count(k)
-    this, prior, last = factors
+    later, prior = factors
 
     def spec(source, wanted=None):
         size, start = g.count(source), g.first(source)
@@ -285,9 +285,9 @@
 
         @pl.when(i == 0)
         def _():
-            bh[...], bl[...] = split(q1[0].T[:half])
+            bh[...], bl[...] = split(q1[0, 0].T[:half])
             th[...], tl[...] = split(qp[0].T)
-            qh[...], ql[...] = split(q2[0].T)
+            qh[...], ql[...] = split(q2[0, 0].T)
 
         @pl.when(c < r)
         def _():
@@ -302,15 +302,23 @@
             do_top = (r > 0) & flag(s, g, 1, r - 1)
             do_bottom = (r < g.N - 1) & (c > r) & flag(s, g, 1, r)
 
-            def top(pair):
-                upper = jnp.concatenate([pair[0][0], pair[1][0]], axis=1)
+            def chosen(here, there, edge, has):
+                pair = [ref[0] for ref in here]
+                if has:
+                    pair = [jnp.where(edge, far[0], near) for far, near in zip(there, pair)]
+                return jnp.concatenate(pair, axis=1)
+
+            @pl.when(do_top)
+            def _():
+                upper = chosen(above_here, above_prev, top_edge(s), has_prev)
                 lower = jnp.concatenate([lt[0], rt[0]], axis=1)
                 y = mul((th[...], tl[...]), split(jnp.concatenate([upper, lower], axis=0)))
                 x[:half, :] = y
 
-            def bottom(pair):
+            @pl.when(do_bottom)
+            def _():
                 upper = jnp.concatenate([lb[0], rb[0]], axis=1)
-                lower = jnp.concatenate([pair[0][0], pair[1][0]], axis=1)
+                lower = chosen(below_here, below_next, bottom_edge(s), has_next)
                 y = mul((bh[...], bl[...]), split(jnp.concatenate([upper, lower], axis=0)))
                 x[half:, half:] = y[:, half:]
 
@@ -318,15 +326,6 @@
                 def _():
                     x[half:, :half] = y[:, :half]
 
-            edge = top_edge(s)
-            if has_prev:
-                pl.when(do_top & edge)(lambda: top(above_prev))
-            pl.when(do_top & jnp.logical_not(edge))(lambda: top(above_here))
-            edge = bottom_edge(s)
-            if has_next:
-                pl.when(do_bottom & edge)(lambda: bottom(below_next))
-            pl.when(do_bottom & jnp.logical_not(edge))(lambda: bottom(below_here))
-
             @pl.when(c == r)
             def _():
                 x[:, :half] = h_ref[:, :half]
@@ -345,17 +344,16 @@
             def _():
                 o_ref[...] = x[...]
 
-    const = lambda i, s: (k, 0, 0)
     column = pl.BlockSpec((1, W, W), lambda i, s: (lo_m + i, 0, 0))
-    operands = [matrix, this, prior, last, col_hi, col_lo, *own, *below[0], *above[0]]
+    operands = [matrix, later, prior, later, col_hi, col_lo, *own, *below[0], *above[0]]
     in_specs = [
         pl.BlockSpec((W, W), lambda i, s: (k, lo_m + i)),
-        pl.BlockSpec((1, W, W), const),
+        pl.BlockSpec((1, 1, W, W), lambda i, s: (0, k, 0, 0)),
         pl.BlockSpec(
             (1, W, half),
             lambda i, s: (jnp.maximum(k - jnp.where(s[0] == 0, 1, 0), 0), 0, 0),
         ),
-        pl.BlockSpec((1, W, W), const),
+        pl.BlockSpec((1, 1, W, W), lambda i, s: (1, k, 0, 0)),
         column,
         column,
         spec(k),
@@ -412,13 +410,18 @@
     ]
     part = g.win // C
 
-    row_factor, col_factor = [], []
-    for f in range(phases):
-        row_factor.append(lax.all_gather(factors[f], "col", axis=1, tiled=True))
+    first = lax.all_gather(factors[:1], "col", axis=2, tiled=True)
+    odd_last = lax.all_gather(factors[1:], "col", axis=2, tiled=True)
+
+    def columns(source, at, since=None):
         cut = [
-            lax.dynamic_slice_in_dim(row_factor[f], (q + d) % C * part, part, axis=1)
+            lax.dynamic_slice(
+                source, (at, 0, (q + d) % C * part, 0), (1, g.kb, part, g.win)
+            )[0]
             for d in range(C)
         ]
+        if since is not None:
+            *cut, _ = lax.optimization_barrier((*cut, since[0, :8, :128]))
         piece = jnp.where(p % C == q, cut[0], 0.0)
         for d in range(1, C):
             piece = piece + lax.ppermute(cut[d], ("row", "col"), spread[d])
@@ -427,17 +430,23 @@
             same.append(swap(piece, "row", j))
         same = jnp.stack(same)
         other = swap(same, "row", 1)
-        col_factor.append(column_factors(g, scalars, same, other))
-    prior = ring(row_factor[1][:, :, g.half :], "row", 1)
+        return column_factors(g, scalars, same, other)
+
+    col_factor = [columns(first, 0), columns(odd_last, 0)]
+    prior = ring(odd_last[0, :, :, g.half :], "row", 1)
 
     own, tops, bottoms = [], [], []
     for k in range(g.kb):
-        left, later, right = even_first(g, k, scalars, hessenberg, row_factor[0], *col_factor[0])
+        left, later, right = even_first(
+            g, k, scalars, hessenberg, first, *col_factor[0]
+        )
         beyond = along(left, "col", -1)
         round_end = around(later, "col", -1)
         lt, lb, lt_end, lb_end, rt, rb = odd_right(
             g, k, scalars, right, beyond, round_end, *col_factor[1]
         )
+        if k == 0:
+            col_factor.append(columns(odd_last, 1, rb))
         lt = along(lt, "col", 1)
         lb = along(lb, "col", 1)
         lt_end = around(lt_end, "col", 1)
@@ -459,7 +468,7 @@
             k,
             scalars,
             hessenberg,
-            (row_factor[1], prior, row_factor[2]),
+            (odd_last, prior),
             *col_factor[2],
             own[k],
             below,

time: 1110 us -> 1060 us (0.955)
  the two profiles are of different devices: /device:TPU:20 before, /device:TPU:0 now
where the time goes in v2:
time: 1060 us; the launch traced here: 1050 us
  waiting for transfers between devices  685 us (65%)
  Pallas kernels  194 us (18%)
  starting transfers between devices  103 us (10%)
  other arithmetic  34.5 us (3%)
  local copies, waits for them, and re-layouts  21 us (2%)
  between operations  14.3 us (1%)
    ppermute x12, waiting for transfers between devices, around(): return lax.ppermute(value, axis, [(last, 0) if steps > 0 else (0, last)])  211 us
    ppermute x12, waiting for transfers between devices, along(): return lax.ppermute(value, axis, pairs)  105 us
    ppermute x17, waiting for transfers between devices, ring(): lax.ppermute(value, axis, [(s, (s + steps) % size) for s in range(size)])  82.3 us
    all_gather x1, waiting for transfers between devices, local(): first = lax.all_gather(factors[:1], 'col', axis=2, tiled=True)  81.9 us
    all_gather x1, waiting for transfers between devices, local(): odd_last = lax.all_gather(factors[1:], 'col', axis=2, tiled=True)  71.2 us
    ppermute x9, waiting for transfers between devices, columns(): piece = piece + lax.ppermute(cut[d], ('row', 'col'), spread[d])  69 us
    pallas_call x4, Pallas kernels, finish(): call(kernel, n, in_specs, pl.BlockSpec((W, W), lambda i, s: (k, lo_m + i)...  66.9 us
    ppermute x12, waiting for transfers between devices, swap(): return lax.ppermute(value, axis, [(s, s ^ bit) for s in range(size)])  64.5 us
  transfers between devices with their start and end apart: 64, of which 32 were waited for; matrix products, arithmetic and copies ran while one was open for 5% of the time, Pallas kernels for 18%

profile of v2, /device:TPU:0, one launch (start us, length us, event | category | flops | bytes accessed | tf_op | source)
XLA Modules:
  0.0 1051.5 jit_solution(2198338572883435819)
XLA Ops:
  10.7 81.9 %all-gather.5.cloned.1.call-done.q_ref = f32[1,4,512,512]{3,2,1,0:T(8,128)} async-done(((f32[1,4,128,512]{3,2,1,0:T(8,128)}), f32[1,4,512,512]{3,2,1,0:T(8,128)}) %all-gather.5.cloned.1.call-update) | async-done | bytes 4194320 | tf_op jit(solution)/shard_map/all_gather | solution.py:413
  102.0 10.2 collective-permute-done.10
  112.2 16.5 %collective-permute-done.9 = f32[4,128,512]{2,1,0:T(8,128)} collective-permute-done((f32[4,128,512]{2,1,0:T(8,128)S(1)}, f32[4,128,512]{2,1,0:T(8,128)}, u32[]{:S(2)}, u32[]{:S(2)}) %collective-permute-start.9) | collective-permute-done | bytes 1048608 | tf_op jit(solution)/shard_map/ppermute | solution.py:427
  136.0 21.2 %collective-permute-done.13 = f32[4,128,512]{2,1,0:T(8,128)S(1)} collective-permute-done((f32[4,128,512]{2,1,0:T(8,128)S(1)}, f32[4,128,512]{2,1,0:T(8,128)S(1)}, u32[]{:S(2)}, u32[]{:S(2)}) %collective-permute-start.13) | collective-permute-done | bytes 1048608 | tf_op jit(solution)/shard_map/ppermute | solution.py:84
  157.2 6.5 collective-permute-done.12
  171.1 71.2 %all-gather.3.cloned.1.call-done.q1.q2 = f32[2,4,512,512]{3,2,1,0:T(8,128)} async-done(((f32[2,4,128,512]{3,2,1,0:T(8,128)}), f32[2,4,512,512]{3,2,1,0:T(8,128)}) %all-gather.3.cloned.1.call-update) | async-done | bytes 8388624 | tf_op jit(solution)/shard_map/all_gather | solution.py:414
  242.3 5.8 dynamic-slice_bitcast_fusion.2
  256.9 7.2 collective-permute-done.19
  264.1 4.8 collective-permute-start.3
  268.9 11.3 %collective-permute-done.18 = f32[4,128,512]{2,1,0:T(8,128)S(1)} collective-permute-done((f32[4,128,512]{2,1,0:T(8,128)S(1)}, f32[4,128,512]{2,1,0:T(8,128)S(1)}, u32[]{:S(2)}, u32[]{:S(2)}) %collective-permute-start.18) | collective-permute-done | bytes 1048608 | tf_op jit(solution)/shard_map/ppermute | solution.py:427
  287.7 8.1 shard_map.47
  295.7 7.0 collective-permute-done.2
  303.7 16.7 %collective-permute-done.3 = f32[4,128,512]{2,1,0:T(8,128)} collective-permute-done((f32[4,128,512]{2,1,0:T(8,128)}, f32[4,128,512]{2,1,0:T(8,128)}, u32[]{:S(2)}, u32[]{:S(2)}) %collective-permute-start.3) | collective-permute-done | bytes 1048608 | tf_op jit(solution)/shard_map/ppermute | solution.py:427
  322.9 13.8 %collective-permute-done.22 = f32[4,128,512]{2,1,0:T(8,128)} collective-permute-done((f32[4,128,512]{2,1,0:T(8,128)S(1)}, f32[4,128,512]{2,1,0:T(8,128)}, u32[]{:S(2)}, u32[]{:S(2)}) %collective-permute-start.22) | collective-permute-done | bytes 1048608 | tf_op jit(solution)/shard_map/ppermute | solution.py:84
  336.7 17.4 %collective-permute-done.20 = f32[4,128,512]{2,1,0:T(8,128)} collective-permute-done((f32[4,128,512]{2,1,0:T(8,128)S(1)}, f32[4,128,512]{2,1,0:T(8,128)}, u32[]{:S(2)}, u32[]{:S(2)}) %collective-permute-start.20) | collective-permute-done | bytes 1048608 | tf_op jit(solution)/shard_map/ppermute | solution.py:84
  358.5 6.5 shard_map.48
  365.0 4.8 collective-permute-start.16
  369.8 10.5 shard_map.51
  382.0 8.7 collective-permute-start.33
  396.4 18.0 %shard_map.55 = (f32[8,512,256]{2,1,0:T(8,128)}, f32[7,512,256]{2,1,0:T(8,128)}, f32[8,512,256]{2,1,0:T(8,128)}) custom-call(s32[98]{0:T(128)} %pad_add_fusion.8.s, f32[2048,4096]{1,0:T(8,128)} %h_ref.17, f32[1,4,512,512]{3,2,1,0:T(8,128)} %all-gather.5.cloned.1.call-done.q_ref, bf16[8,512,512]{2,1,0:T(8,128)(2,1)} %get-tuple-element.57.ch, ...), custom_call_target="tpu_custom_call" | custom-call | flops 12884901888 | bytes 25165824 | tf_op jit(solution)/shard_map/pallas_call | solution.py:175
  418.9 33.1 %collective-permute-done.15.b_ref = f32[2,512,256]{2,1,0:T(8,128)} collective-permute-done((f32[2,512,256]{2,1,0:T(8,128)}, f32[2,512,256]{2,1,0:T(8,128)}, u32[]{:S(2)}, u32[]{:S(2)}) %collective-permute-start.15) | collective-permute-done | bytes 1048608 | tf_op jit(solution)/shard_map/ppermute | solution.py:74
  452.0 5.2 collective-permute-start.53
  458.5 12.4 %shard_map.53 = (f32[6,512,256]{2,1,0:T(8,128)}, f32[5,512,256]{2,1,0:T(8,128)}, f32[6,512,256]{2,1,0:T(8,128)}) custom-call(s32[98]{0:T(128)} %pad_add_fusion.8.s, f32[2048,4096]{1,0:T(8,128)} %h_ref.17, f32[1,4,512,512]{3,2,1,0:T(8,128)} %all-gather.5.cloned.1.call-done.q_ref, bf16[8,512,512]{2,1,0:T(8,128)(2,1)} %get-tuple-element.57.ch, ...), custom_call_target="tpu_custom_call" | custom-call | flops 9663676416 | bytes 18874368 | tf_op jit(solution)/shard_map/pallas_call | solution.py:175
  472.3 9.6 collective-permute-start.43
  481.9 8.1 shard_map.49
  490.0 5.6 shard_map.50
  495.6 93.9 %collective-permute-done.43.e_ref = f32[5,512,256]{2,1,0:T(8,128)} collective-permute-done((f32[5,512,256]{2,1,0:T(8,128)}, f32[5,512,256]{2,1,0:T(8,128)}, u32[]{:S(2)}, u32[]{:S(2)}) %collective-permute-start.43) | collective-permute-done | bytes 2621472 | tf_op jit(solution)/shard_map/ppermute | solution.py:79
  590.8 26.7 %collective-permute-done.42.b_ref = f32[6,512,256]{2,1,0:T(8,128)} collective-permute-done((f32[6,512,256]{2,1,0:T(8,128)}, f32[6,512,256]{2,1,0:T(8,128)}, u32[]{:S(2)}, u32[]{:S(2)}) %collective-permute-start.42) | collective-permute-done | bytes 3145760 | tf_op jit(solution)/shard_map/ppermute | solution.py:74
  619.0 9.2 shard_map.52
  632.2 12.3 %shard_map.54 = (f32[6,256,256]{2,1,0:T(8,128)}, f32[6,256,256]{2,1,0:T(8,128)}, f32[5,256,256]{2,1,0:T(8,128)}, f32[5,256,256]{2,1,0:T(8,128)}, f32[6,256,256]{2,1,0:T(8,128)}, /*index=5*/f32[6,256,256]{2,1,0:T(8,128)}) custom-call(s32[98]{0:T(128)} %pad_add_fusion.8.s, f32[6,512,256]{2,1,0:T(8,128)} %get-tuple-element.79.r_ref, ...), custom_call_target="tpu_custom_call" | custom-call | flops 4831838208 | bytes 18874368 | tf_op jit(solution)/shard_map/pallas_call | solution.py:235
  653.6 14.8 %shard_map.56 = (f32[8,256,256]{2,1,0:T(8,128)}, f32[8,256,256]{2,1,0:T(8,128)}, f32[7,256,256]{2,1,0:T(8,128)}, f32[7,256,256]{2,1,0:T(8,128)}, f32[8,256,256]{2,1,0:T(8,128)}, /*index=5*/f32[8,256,256]{2,1,0:T(8,128)}) custom-call(s32[98]{0:T(128)} %pad_add_fusion.8.s, f32[8,512,256]{2,1,0:T(8,128)} %get-tuple-element.88.r_ref, ...), custom_call_target="tpu_custom_call" | custom-call | flops 6442450944 | bytes 25165824 | tf_op jit(solution)/shard_map/pallas_call | solution.py:235
  669.7 10.8 %collective-permute-done.39 = f32[3,256,256]{2,1,0:T(8,128)} collective-permute-done((f32[3,256,256]{2,1,0:T(8,128)}, f32[3,256,256]{2,1,0:T(8,128)}, u32[]{:S(2)}, u32[]{:S(2)}) %collective-permute-start.39) | collective-permute-done | bytes 786464 | tf_op jit(solution)/shard_map/ppermute | solution.py:79
  683.3 11.7 %collective-permute-done.38 = f32[4,256,256]{2,1,0:T(8,128)S(1)} collective-permute-done((f32[4,256,256]{2,1,0:T(8,128)}, f32[4,256,256]{2,1,0:T(8,128)S(1)}, u32[]{:S(2)}, u32[]{:S(2)}) %collective-permute-start.38) | collective-permute-done | bytes 1048608 | tf_op jit(solution)/shard_map/ppermute | solution.py:74
  699.4 9.1 collective-permute-done.45
  709.8 66.1 %collective-permute-done.49 = f32[5,256,256]{2,1,0:T(8,128)S(1)} collective-permute-done((f32[5,256,256]{2,1,0:T(8,128)}, f32[5,256,256]{2,1,0:T(8,128)S(1)}, u32[]{:S(2)}, u32[]{:S(2)}) %collective-permute-start.49) | collective-permute-done | bytes 1310752 | tf_op jit(solution)/shard_map/ppermute | solution.py:79
  781.6 29.4 %collective-permute-done.59 = f32[7,256,256]{2,1,0:T(8,128)S(1)} collective-permute-done((f32[7,256,256]{2,1,0:T(8,128)}, f32[7,256,256]{2,1,0:T(8,128)S(1)}, u32[]{:S(2)}, u32[]{:S(2)}) %collective-permute-start.59) | collective-permute-done | bytes 1835040 | tf_op jit(solution)/shard_map/ppermute | solution.py:79
  818.6 30.3 %collective-permute-done.48 = f32[6,256,256]{2,1,0:T(8,128)S(1)} collective-permute-done((f32[6,256,256]{2,1,0:T(8,128)}, f32[6,256,256]{2,1,0:T(8,128)S(1)}, u32[]{:S(2)}, u32[]{:S(2)}) %collective-permute-start.48) | collective-permute-done | bytes 1572896 | tf_op jit(solution)/shard_map/ppermute | solution.py:74
  851.4 13.9 %shard_map.57.rest_6_ = f32[2048,4096]{1,0:T(8,128)} custom-call(s32[24]{0:T(128)} %constant.91.s, f32[2048,4096]{1,0:T(8,128)} %h_ref.17), custom_call_target="tpu_custom_call" | custom-call | flops 3145728 | bytes 25165824 | tf_op jit(solution)/shard_map/pallas_call | solution.py:128
  865.3 8.2 shard_map.46
  884.9 36.8 %collective-permute-done.50.rest_4_.rest_0_ = f32[6,256,256]{2,1,0:T(8,128)} collective-permute-done((f32[6,256,256]{2,1,0:T(8,128)}, f32[6,256,256]{2,1,0:T(8,128)}, u32[]{:S(2)}, u32[]{:S(2)}) %collective-permute-start.50) | collective-permute-done | bytes 1572896 | tf_op jit(solution)/shard_map/ppermute | solution.py:68
  924.6 22.4 %shard_map.58.rest_8_ = f32[2048,4096]{1,0:T(8,128)} custom-call(s32[98]{0:T(128)} %pad_add_fusion.8.s, f32[2048,4096]{1,0:T(8,128)} %h_ref.17, f32[2,4,512,512]{3,2,1,0:T(8,128)} %all-gather.3.cloned.1.call-done.q1.q2, f32[4,512,256]{2,1,0:T(8,128)} %copy-done, ...), custom_call_target="tpu_custom_call", output_to_operand_aliasing={{}: (17, {})} | custom-call | flops 19327352832 | bytes 50331648 | tf_op jit(solution)/shard_map/pallas_call | solution.py:377
  946.9 7.2 collective-permute-done.41.rest_5_.rest_1_
  959.8 16.8 %collective-permute-done.40.rest_4_.rest_0_ = f32[4,256,256]{2,1,0:T(8,128)} collective-permute-done((f32[4,256,256]{2,1,0:T(8,128)}, f32[4,256,256]{2,1,0:T(8,128)}, u32[]{:S(2)}, u32[]{:S(2)}) %collective-permute-start.40) | collective-permute-done | bytes 1048608 | tf_op jit(solution)/shard_map/ppermute | solution.py:68
  979.4 9.9 collective-permute-done.46.rest_2_.rest_6_
  989.3 19.3 %shard_map.59.rest_8_ = f32[2048,4096]{1,0:T(8,128)} custom-call(s32[98]{0:T(128)} %pad_add_fusion.8.s, f32[2048,4096]{1,0:T(8,128)} %h_ref.17, f32[2,4,512,512]{3,2,1,0:T(8,128)} %all-gather.3.cloned.1.call-done.q1.q2, f32[4,512,256]{2,1,0:T(8,128)} %copy-done, ...), custom_call_target="tpu_custom_call", output_to_operand_aliasing={{}: (19, {})} | custom-call | flops 14495514624 | bytes 37748736 | tf_op jit(solution)/shard_map/pallas_call | solution.py:377
  1010.3 7.0 collective-permute-done.36.rest_2_.rest_4_
  1018.3 15.7 %shard_map.60.rest_6_ = f32[2048,4096]{1,0:T(8,128)} custom-call(s32[98]{0:T(128)} %pad_add_fusion.8.s, f32[2048,4096]{1,0:T(8,128)} %h_ref.17, f32[2,4,512,512]{3,2,1,0:T(8,128)} %all-gather.3.cloned.1.call-done.q1.q2, f32[4,512,256]{2,1,0:T(8,128)} %copy-done, ...), custom_call_target="tpu_custom_call", output_to_operand_aliasing={{}: (19, {})} | custom-call | flops 9663676416 | bytes 25165824 | tf_op jit(solution)/shard_map/pallas_call | solution.py:377
  1034.8 9.6 shard_map.61
  (161 shorter events, 134.2 us)
Async XLA Ops:
  6.5 86.1 %all-gather.5.cloned.1.call-start = ((), (), s32[]{:S(2)}) async-start(), calls=%async_computation.1 | async-start | bytes 5242880 | tf_op jit(solution)/shard_map/all_gather | solution.py:413
  9.0 233.3 %all-gather.3.cloned.1.call-start = ((), (), s32[]{:S(2)}) async-start(), calls=%async_computation | async-start | bytes 10485760 | tf_op jit(solution)/shard_map/all_gather | solution.py:414
  135.3 33.1 %collective-permute-start.11 = (f32[4,128,512]{2,1,0:T(8,128)S(1)}, f32[4,128,512]{2,1,0:T(8,128)S(1)}, u32[]{:S(2)}, u32[]{:S(2)}) collective-permute-start(f32[4,128,512]{2,1,0:T(8,128)S(1)} %fusion.3), channel_id=1, source_target_pairs={{0,8},{4,12},{8,0},{12,4},{16,24},{20,28},{24,16},{28,20},{1,9},{5... | collective-permute-start | bytes 3145736 | tf_op jit(solution)/shard_map/ppermute | solution.py:84
  171.1 115.2 %collective-permute-start.14 = (f32[4,4,128,512]{3,2,1,0:T(8,128)}, f32[4,4,128,512]{3,2,1,0:T(8,128)}, u32[]{:S(2)}, u32[]{:S(2)}) collective-permute-start(f32[4,4,128,512]{3,2,1,0:T(8,128)} %pad_maximum_fusion.1.same_ref), channel_id=1, source_target_pairs={{0,4},{4,0},{8,12},{12,8},{16,20},{20,16},{24,28},{28,24},{1,5},{5... | collective-permute-start | bytes 12582920 | tf_op jit(solution)/shard_map/ppermute | solution.py:84
  255.6 47.2 %collective-permute-start.2 = (f32[4,128,512]{2,1,0:T(8,128)}, f32[4,128,512]{2,1,0:T(8,128)S(1)}, u32[]{:S(2)}, u32[]{:S(2)}) collective-permute-start(f32[4,128,512]{2,1,0:T(8,128)} %get-tuple-element.53), channel_id=1, source_target_pairs={{0,8},{5,13},{10,2},{15,7},{16,24},{21,29},{26,18},{31,23}} | collective-permute-start | bytes 3145736 | tf_op jit(solution)/shard_map/ppermute | solution.py:427
  264.1 56.3 %collective-permute-start.3 = (f32[4,128,512]{2,1,0:T(8,128)}, f32[4,128,512]{2,1,0:T(8,128)}, u32[]{:S(2)}, u32[]{:S(2)}) collective-permute-start(f32[4,128,512]{2,1,0:T(8,128)} %get-tuple-element.54), channel_id=1, source_target_pairs={{0,12},{5,1},{10,6},{15,11},{16,28},{21,17},{26,22},{31,27}} | collective-permute-start | bytes 3145736 | tf_op jit(solution)/shard_map/ppermute | solution.py:427
  281.9 54.7 %collective-permute-start.22 = (f32[4,128,512]{2,1,0:T(8,128)S(1)}, f32[4,128,512]{2,1,0:T(8,128)}, u32[]{:S(2)}, u32[]{:S(2)}) collective-permute-start(f32[4,128,512]{2,1,0:T(8,128)S(1)} %fusion.1), channel_id=1, source_target_pairs={{0,24},{4,28},{8,16},{12,20},{16,8},{20,12},{24,0},{28,4},{1,25},{... | collective-permute-start | bytes 3145736 | tf_op jit(solution)/shard_map/ppermute | solution.py:84
  286.3 50.4 %collective-permute-start.21 = (f32[4,128,512]{2,1,0:T(8,128)S(1)}, f32[4,128,512]{2,1,0:T(8,128)}, u32[]{:S(2)}, u32[]{:S(2)}) collective-permute-start(f32[4,128,512]{2,1,0:T(8,128)S(1)} %fusion.1), channel_id=1, source_target_pairs={{0,16},{4,20},{8,24},{12,28},{16,0},{20,4},{24,8},{28,12},{1,17},{... | collective-permute-start | bytes 3145736 | tf_op jit(solution)/shard_map/ppermute | solution.py:84
  286.3 67.7 %collective-permute-start.20 = (f32[4,128,512]{2,1,0:T(8,128)S(1)}, f32[4,128,512]{2,1,0:T(8,128)}, u32[]{:S(2)}, u32[]{:S(2)}) collective-permute-start(f32[4,128,512]{2,1,0:T(8,128)S(1)} %fusion.1), channel_id=1, source_target_pairs={{0,8},{4,12},{8,0},{12,4},{16,24},{20,28},{24,16},{28,20},{1,9},{5... | collective-permute-start | bytes 3145736 | tf_op jit(solution)/shard_map/ppermute | solution.py:84
  322.8 59.2 %collective-permute-start.6 = (f32[4,128,512]{2,1,0:T(8,128)S(1)}, f32[4,128,512]{2,1,0:T(8,128)S(1)}, u32[]{:S(2)}, u32[]{:S(2)}) collective-permute-start(f32[4,128,512]{2,1,0:T(8,128)S(1)} %add_add_fusion), channel_id=1, source_target_pairs={{0,24},{4,28},{8,16},{12,20},{16,8},{20,12},{24,0},{28,4},{1,25},{... | collective-permute-start | bytes 3145736 | tf_op jit(solution)/shard_map/ppermute | solution.py:84
  358.5 113.8 %collective-permute-start.23 = (f32[4,4,128,512]{3,2,1,0:T(8,128)}, f32[4,4,128,512]{3,2,1,0:T(8,128)}, u32[]{:S(2)}, u32[]{:S(2)}) collective-permute-start(f32[4,4,128,512]{3,2,1,0:T(8,128)} %pad_maximum_fusion.2.same_ref), channel_id=1, source_target_pairs={{0,4},{4,0},{8,12},{12,8},{16,20},{20,16},{24,28},{28,24},{1,5},{5... | collective-permute-start | bytes 12582920 | tf_op jit(solution)/shard_map/ppermute | solution.py:84
  380.7 77.8 %collective-permute-start.32 = (f32[4,512,256]{2,1,0:T(8,128)}, f32[4,512,256]{2,1,0:T(8,128)}, u32[]{:S(2)}, u32[]{:S(2)}) collective-permute-start(f32[4,512,256]{2,1,0:T(8,128)} %get-tuple-element.71), channel_id=1, source_target_pairs={{1,0},{2,1},{3,2},{5,4},{6,5},{7,6},{9,8},{10,9},{11,10},{13,12},{... | collective-permute-start | bytes 6291464 | tf_op jit(solution)/shard_map/ppermute | solution.py:74
  382.0 75.2 %collective-permute-start.33 = (f32[3,512,256]{2,1,0:T(8,128)}, f32[3,512,256]{2,1,0:T(8,128)}, u32[]{:S(2)}, u32[]{:S(2)}) collective-permute-start(f32[3,512,256]{2,1,0:T(8,128)} %get-tuple-element.72), channel_id=1, source_target_pairs={{0,3},{4,7},{8,11},{12,15},{16,19},{20,23},{24,27},{28,31}} | collective-permute-start | bytes 4718600 | tf_op jit(solution)/shard_map/ppermute | solution.py:79
  394.6 57.4 %collective-permute-start.15 = (f32[2,512,256]{2,1,0:T(8,128)}, f32[2,512,256]{2,1,0:T(8,128)}, u32[]{:S(2)}, u32[]{:S(2)}) collective-permute-start(f32[2,512,256]{2,1,0:T(8,128)} %get-tuple-element.60), channel_id=1, source_target_pairs={{1,0},{2,1},{3,2},{5,4},{6,5},{7,6},{9,8},{10,9},{11,10},{13,12},{... | collective-permute-start | bytes 3145736 | tf_op jit(solution)/shard_map/ppermute | solution.py:74
  395.9 75.1 %collective-permute-start = (f32[4,512,256]{2,1,0:T(8,128)}, f32[4,512,256]{2,1,0:T(8,128)S(1)}, u32[]{:S(2)}, u32[]{:S(2)}) collective-permute-start(f32[4,512,256]{2,1,0:T(8,128)} %slice_bitcast_fusion), channel_id=1, source_target_pairs={{0,4},{4,8},{8,12},{12,16},{16,20},{20,24},{24,28},{28,0},{1,5},{5... | collective-permute-start | bytes 6291464 | tf_op jit(solution)/shard_map/ppermute | solution.py:68
  452.0 176.2 %collective-permute-start.53 = (f32[7,512,256]{2,1,0:T(8,128)}, f32[7,512,256]{2,1,0:T(8,128)}, u32[]{:S(2)}, u32[]{:S(2)}) collective-permute-start(f32[7,512,256]{2,1,0:T(8,128)} %get-tuple-element.90), channel_id=1, source_target_pairs={{0,3},{4,7},{8,11},{12,15},{16,19},{20,23},{24,27},{28,31}} | collective-permute-start | bytes 11010056 | tf_op jit(solution)/shard_map/ppermute | solution.py:79
  457.2 172.4 %collective-permute-start.52 = (f32[8,512,256]{2,1,0:T(8,128)}, f32[8,512,256]{2,1,0:T(8,128)}, u32[]{:S(2)}, u32[]{:S(2)}) collective-permute-start(f32[8,512,256]{2,1,0:T(8,128)} %get-tuple-element.89), channel_id=1, source_target_pairs={{1,0},{2,1},{3,2},{5,4},{6,5},{7,6},{9,8},{10,9},{11,10},{13,12},{... | collective-permute-start | bytes 12582920 | tf_op jit(solution)/shard_map/ppermute | solution.py:74
  458.5 172.4 %collective-permute-start.7 = (f32[4,4,128,512]{3,2,1,0:T(8,128)}, f32[4,4,128,512]{3,2,1,0:T(8,128)}, u32[]{:S(2)}, u32[]{:S(2)}) collective-permute-start(f32[4,4,128,512]{3,2,1,0:T(8,128)} %pad_maximum_fusion.same_ref), channel_id=1, source_target_pairs={{0,4},{4,0},{8,12},{12,8},{16,20},{20,16},{24,28},{28,24},{1,5},{5... | collective-permute-start | bytes 12582920 | tf_op jit(solution)/shard_map/ppermute | solution.py:84
  471.0 146.6 %collective-permute-start.42 = (f32[6,512,256]{2,1,0:T(8,128)}, f32[6,512,256]{2,1,0:T(8,128)}, u32[]{:S(2)}, u32[]{:S(2)}) collective-permute-start(f32[6,512,256]{2,1,0:T(8,128)} %get-tuple-element.80), channel_id=1, source_target_pairs={{1,0},{2,1},{3,2},{5,4},{6,5},{7,6},{9,8},{10,9},{11,10},{13,12},{... | collective-permute-start | bytes 9437192 | tf_op jit(solution)/shard_map/ppermute | solution.py:74
  472.3 117.3 %collective-permute-start.43 = (f32[5,512,256]{2,1,0:T(8,128)}, f32[5,512,256]{2,1,0:T(8,128)}, u32[]{:S(2)}, u32[]{:S(2)}) collective-permute-start(f32[5,512,256]{2,1,0:T(8,128)} %get-tuple-element.81), channel_id=1, source_target_pairs={{0,3},{4,7},{8,11},{12,15},{16,19},{20,23},{24,27},{28,31}} | collective-permute-start | bytes 7864328 | tf_op jit(solution)/shard_map/ppermute | solution.py:79
  589.5 59.2 %collective-permute-start.24 = (f32[2,256,256]{2,1,0:T(8,128)}, f32[2,256,256]{2,1,0:T(8,128)S(1)}, u32[]{:S(2)}, u32[]{:S(2)}) collective-permute-start(f32[2,256,256]{2,1,0:T(8,128)} %get-tuple-element.64), channel_id=1, source_target_pairs={{0,1},{1,2},{2,3},{4,5},{5,6},{6,7},{8,9},{9,10},{10,11},{12,13},{... | collective-permute-start | bytes 1572872 | tf_op jit(solution)/shard_map/ppermute | solution.py:74
  617.5 33.9 %collective-permute-start.26 = (f32[2,256,256]{2,1,0:T(8,128)}, f32[2,256,256]{2,1,0:T(8,128)S(1)}, u32[]{:S(2)}, u32[]{:S(2)}) collective-permute-start(f32[2,256,256]{2,1,0:T(8,128)} %get-tuple-element.66), channel_id=1, source_target_pairs={{0,1},{1,2},{2,3},{4,5},{5,6},{6,7},{8,9},{9,10},{10,11},{12,13},{... | collective-permute-start | bytes 1572872 | tf_op jit(solution)/shard_map/ppermute | solution.py:74
  630.9 37.5 %collective-permute-start.35 = (f32[3,256,256]{2,1,0:T(8,128)}, f32[3,256,256]{2,1,0:T(8,128)}, u32[]{:S(2)}, u32[]{:S(2)}) collective-permute-start(f32[3,256,256]{2,1,0:T(8,128)} %get-tuple-element.74), channel_id=1, source_target_pairs={{3,0},{7,4},{11,8},{15,12},{19,16},{23,20},{27,24},{31,28}} | collective-permute-start | bytes 2359304 | tf_op jit(solution)/shard_map/ppermute | solution.py:79
  644.5 36.1 %collective-permute-start.39 = (f32[3,256,256]{2,1,0:T(8,128)}, f32[3,256,256]{2,1,0:T(8,128)}, u32[]{:S(2)}, u32[]{:S(2)}) collective-permute-start(f32[3,256,256]{2,1,0:T(8,128)} %get-tuple-element.77), channel_id=1, source_target_pairs={{3,0},{7,4},{11,8},{15,12},{19,16},{23,20},{27,24},{31,28}} | collective-permute-start | bytes 2359304 | tf_op jit(solution)/shard_map/ppermute | solution.py:79
  646.7 35.2 %collective-permute-start.34 = (f32[4,256,256]{2,1,0:T(8,128)}, f32[4,256,256]{2,1,0:T(8,128)S(1)}, u32[]{:S(2)}, u32[]{:S(2)}) collective-permute-start(f32[4,256,256]{2,1,0:T(8,128)} %get-tuple-element.73), channel_id=1, source_target_pairs={{0,1},{1,2},{2,3},{4,5},{5,6},{6,7},{8,9},{9,10},{10,11},{12,13},{... | collective-permute-start | bytes 3145736 | tf_op jit(solution)/shard_map/ppermute | solution.py:74
  649.5 45.4 %collective-permute-start.38 = (f32[4,256,256]{2,1,0:T(8,128)}, f32[4,256,256]{2,1,0:T(8,128)S(1)}, u32[]{:S(2)}, u32[]{:S(2)}) collective-permute-start(f32[4,256,256]{2,1,0:T(8,128)} %get-tuple-element.76), channel_id=1, source_target_pairs={{0,1},{1,2},{2,3},{4,5},{5,6},{6,7},{8,9},{9,10},{10,11},{12,13},{... | collective-permute-start | bytes 3145736 | tf_op jit(solution)/shard_map/ppermute | solution.py:74
  652.3 56.2 %collective-permute-start.45 = (f32[5,256,256]{2,1,0:T(8,128)}, f32[5,256,256]{2,1,0:T(8,128)S(1)}, u32[]{:S(2)}, u32[]{:S(2)}) collective-permute-start(f32[5,256,256]{2,1,0:T(8,128)} %get-tuple-element.83), channel_id=1, source_target_pairs={{3,0},{7,4},{11,8},{15,12},{19,16},{23,20},{27,24},{31,28}} | collective-permute-start | bytes 3932168 | tf_op jit(solution)/shard_map/ppermute | solution.py:79
  668.4 110.0 %collective-permute-start.55 = (f32[7,256,256]{2,1,0:T(8,128)}, f32[7,256,256]{2,1,0:T(8,128)S(1)}, u32[]{:S(2)}, u32[]{:S(2)}) collective-permute-start(f32[7,256,256]{2,1,0:T(8,128)} %get-tuple-element.92), channel_id=1, source_target_pairs={{3,0},{7,4},{11,8},{15,12},{19,16},{23,20},{27,24},{31,28}} | collective-permute-start | bytes 5505032 | tf_op jit(solution)/shard_map/ppermute | solution.py:79
  680.5 99.2 %collective-permute-start.54 = (f32[8,256,256]{2,1,0:T(8,128)}, f32[8,256,256]{2,1,0:T(8,128)S(1)}, u32[]{:S(2)}, u32[]{:S(2)}) collective-permute-start(f32[8,256,256]{2,1,0:T(8,128)} %get-tuple-element.91), channel_id=1, source_target_pairs={{0,1},{1,2},{2,3},{4,5},{5,6},{6,7},{8,9},{9,10},{10,11},{12,13},{... | collective-permute-start | bytes 6291464 | tf_op jit(solution)/shard_map/ppermute | solution.py:74
  682.0 94.0 %collective-permute-start.49 = (f32[5,256,256]{2,1,0:T(8,128)}, f32[5,256,256]{2,1,0:T(8,128)S(1)}, u32[]{:S(2)}, u32[]{:S(2)}) collective-permute-start(f32[5,256,256]{2,1,0:T(8,128)} %get-tuple-element.86), channel_id=1, source_target_pairs={{3,0},{7,4},{11,8},{15,12},{19,16},{23,20},{27,24},{31,28}} | collective-permute-start | bytes 3932168 | tf_op jit(solution)/shard_map/ppermute | solution.py:79
  695.0 116.0 %collective-permute-start.58 = (f32[8,256,256]{2,1,0:T(8,128)}, f32[8,256,256]{2,1,0:T(8,128)S(1)}, u32[]{:S(2)}, u32[]{:S(2)}) collective-permute-start(f32[8,256,256]{2,1,0:T(8,128)} %get-tuple-element.94), channel_id=1, source_target_pairs={{0,1},{1,2},{2,3},{4,5},{5,6},{6,7},{8,9},{9,10},{10,11},{12,13},{... | collective-permute-start | bytes 6291464 | tf_op jit(solution)/shard_map/ppermute | solution.py:74
  708.5 102.5 %collective-permute-start.59 = (f32[7,256,256]{2,1,0:T(8,128)}, f32[7,256,256]{2,1,0:T(8,128)S(1)}, u32[]{:S(2)}, u32[]{:S(2)}) collective-permute-start(f32[7,256,256]{2,1,0:T(8,128)} %get-tuple-element.95), channel_id=1, source_target_pairs={{3,0},{7,4},{11,8},{15,12},{19,16},{23,20},{27,24},{31,28}} | collective-permute-start | bytes 5505032 | tf_op jit(solution)/shard_map/ppermute | solution.py:79
  775.9 42.7 %collective-permute-start.44 = (f32[6,256,256]{2,1,0:T(8,128)}, f32[6,256,256]{2,1,0:T(8,128)}, u32[]{:S(2)}, u32[]{:S(2)}) collective-permute-start(f32[6,256,256]{2,1,0:T(8,128)} %get-tuple-element.82), channel_id=1, source_target_pairs={{0,1},{1,2},{2,3},{4,5},{5,6},{6,7},{8,9},{9,10},{10,11},{12,13},{... | collective-permute-start | bytes 4718600 | tf_op jit(solution)/shard_map/ppermute | solution.py:74
  778.4 70.5 %collective-permute-start.48 = (f32[6,256,256]{2,1,0:T(8,128)}, f32[6,256,256]{2,1,0:T(8,128)S(1)}, u32[]{:S(2)}, u32[]{:S(2)}) collective-permute-start(f32[6,256,256]{2,1,0:T(8,128)} %get-tuple-element.85), channel_id=1, source_target_pairs={{0,1},{1,2},{2,3},{4,5},{5,6},{6,7},{8,9},{9,10},{10,11},{12,13},{... | collective-permute-start | bytes 4718600 | tf_op jit(solution)/shard_map/ppermute | solution.py:74
  779.8 70.5 %collective-permute-start.51 = (f32[6,256,256]{2,1,0:T(8,128)}, f32[6,256,256]{2,1,0:T(8,128)}, u32[]{:S(2)}, u32[]{:S(2)}) collective-permute-start(f32[6,256,256]{2,1,0:T(8,128)} %get-tuple-element.87.rt), channel_id=1, source_target_pairs={{0,28},{4,0},{8,4},{12,8},{16,12},{20,16},{24,20},{28,24},{1,29},{... | collective-permute-start | bytes 4718600 | tf_op jit(solution)/shard_map/ppermute | solution.py:68
  811.0 73.8 %collective-permute-start.57 = (f32[8,256,256]{2,1,0:T(8,128)}, f32[8,256,256]{2,1,0:T(8,128)S(1)}, u32[]{:S(2)}, u32[]{:S(2)}) collective-permute-start(f32[8,256,256]{2,1,0:T(8,128)} %get-tuple-element.93.rb), channel_id=1, source_target_pairs={{0,4},{4,8},{8,12},{12,16},{16,20},{20,24},{24,28},{28,0},{1,5},{5... | collective-permute-start | bytes 6291464 | tf_op jit(solution)/shard_map/ppermute | solution.py:68
  811.0 73.8 %collective-permute-start.61 = (f32[8,256,256]{2,1,0:T(8,128)}, f32[8,256,256]{2,1,0:T(8,128)}, u32[]{:S(2)}, u32[]{:S(2)}) collective-permute-start(f32[8,256,256]{2,1,0:T(8,128)} %get-tuple-element.96.rt), channel_id=1, source_target_pairs={{0,28},{4,0},{8,4},{12,8},{16,12},{20,16},{24,20},{28,24},{1,29},{... | collective-permute-start | bytes 6291464 | tf_op jit(solution)/shard_map/ppermute | solution.py:68
  818.6 103.8 %collective-permute-start.56 = (f32[8,256,256]{2,1,0:T(8,128)}, f32[8,256,256]{2,1,0:T(8,128)}, u32[]{:S(2)}, u32[]{:S(2)}) collective-permute-start(f32[8,256,256]{2,1,0:T(8,128)} %pad_add_fusion.1.lb), channel_id=1, source_target_pairs={{0,4},{4,8},{8,12},{12,16},{16,20},{20,24},{24,28},{28,0},{1,5},{5... | collective-permute-start | bytes 6291464 | tf_op jit(solution)/shard_map/ppermute | solution.py:68
  848.8 75.7 %collective-permute-start.60 = (f32[8,256,256]{2,1,0:T(8,128)}, f32[8,256,256]{2,1,0:T(8,128)}, u32[]{:S(2)}, u32[]{:S(2)}) collective-permute-start(f32[8,256,256]{2,1,0:T(8,128)} %pad_add_fusion.lt), channel_id=1, source_target_pairs={{0,28},{4,0},{8,4},{12,8},{16,12},{20,16},{24,20},{28,24},{1,29},{... | collective-permute-start | bytes 6291464 | tf_op jit(solution)/shard_map/ppermute | solution.py:68
  850.2 71.5 %collective-permute-start.50 = (f32[6,256,256]{2,1,0:T(8,128)}, f32[6,256,256]{2,1,0:T(8,128)}, u32[]{:S(2)}, u32[]{:S(2)}) collective-permute-start(f32[6,256,256]{2,1,0:T(8,128)} %pad_add_fusion.2.lt), channel_id=1, source_target_pairs={{0,28},{4,0},{8,4},{12,8},{16,12},{20,16},{24,20},{28,24},{1,29},{... | collective-permute-start | bytes 4718600 | tf_op jit(solution)/shard_map/ppermute | solution.py:68
  884.8 123.8 %collective-permute-start.29 = (f32[2,256,256]{2,1,0:T(8,128)}, f32[2,256,256]{2,1,0:T(8,128)}, u32[]{:S(2)}, u32[]{:S(2)}) collective-permute-start(f32[2,256,256]{2,1,0:T(8,128)} %get-tuple-element.68.rt), channel_id=1, source_target_pairs={{0,28},{4,0},{8,4},{12,8},{16,12},{20,16},{24,20},{28,24},{1,29},{... | collective-permute-start | bytes 1572872 | tf_op jit(solution)/shard_map/ppermute | solution.py:68
  884.8 69.4 %collective-permute-start.41 = (f32[4,256,256]{2,1,0:T(8,128)}, f32[4,256,256]{2,1,0:T(8,128)S(1)}, u32[]{:S(2)}, u32[]{:S(2)}) collective-permute-start(f32[4,256,256]{2,1,0:T(8,128)} %get-tuple-element.78.rt), channel_id=1, source_target_pairs={{0,28},{4,0},{8,4},{12,8},{16,12},{20,16},{24,20},{28,24},{1,29},{... | collective-permute-start | bytes 3145736 | tf_op jit(solution)/shard_map/ppermute | solution.py:68
  921.7 38.1 %collective-permute-start.47 = (f32[6,256,256]{2,1,0:T(8,128)}, f32[6,256,256]{2,1,0:T(8,128)}, u32[]{:S(2)}, u32[]{:S(2)}) collective-permute-start(f32[6,256,256]{2,1,0:T(8,128)} %get-tuple-element.84.rb), channel_id=1, source_target_pairs={{0,4},{4,8},{8,12},{12,16},{16,20},{20,24},{24,28},{28,0},{1,5},{5... | collective-permute-start | bytes 4718600 | tf_op jit(solution)/shard_map/ppermute | solution.py:68
  922.3 54.3 %collective-permute-start.40 = (f32[4,256,256]{2,1,0:T(8,128)}, f32[4,256,256]{2,1,0:T(8,128)}, u32[]{:S(2)}, u32[]{:S(2)}) collective-permute-start(f32[4,256,256]{2,1,0:T(8,128)} %pad_add_fusion.4.lt), channel_id=1, source_target_pairs={{0,28},{4,0},{8,4},{12,8},{16,12},{20,16},{24,20},{28,24},{1,29},{... | collective-permute-start | bytes 3145736 | tf_op jit(solution)/shard_map/ppermute | solution.py:68
  924.6 64.8 %collective-permute-start.46 = (f32[6,256,256]{2,1,0:T(8,128)}, f32[6,256,256]{2,1,0:T(8,128)}, u32[]{:S(2)}, u32[]{:S(2)}) collective-permute-start(f32[6,256,256]{2,1,0:T(8,128)} %pad_add_fusion.3.lb), channel_id=1, source_target_pairs={{0,4},{4,8},{8,12},{12,16},{16,20},{20,24},{24,28},{28,0},{1,5},{5... | collective-permute-start | bytes 4718600 | tf_op jit(solution)/shard_map/ppermute | solution.py:68
  954.1 79.8 %collective-permute-start.31 = (f32[2,256,256]{2,1,0:T(8,128)}, f32[2,256,256]{2,1,0:T(8,128)}, u32[]{:S(2)}, u32[]{:S(2)}) collective-permute-start(f32[2,256,256]{2,1,0:T(8,128)} %get-tuple-element.69.rb), channel_id=1, source_target_pairs={{0,4},{4,8},{8,12},{12,16},{16,20},{20,24},{24,28},{28,0},{1,5},{5... | collective-permute-start | bytes 1572872 | tf_op jit(solution)/shard_map/ppermute | solution.py:68
  959.8 50.5 %collective-permute-start.37 = (f32[4,256,256]{2,1,0:T(8,128)}, f32[4,256,256]{2,1,0:T(8,128)S(1)}, u32[]{:S(2)}, u32[]{:S(2)}) collective-permute-start(f32[4,256,256]{2,1,0:T(8,128)} %get-tuple-element.75.rb), channel_id=1, source_target_pairs={{0,4},{4,8},{8,12},{12,16},{16,20},{20,24},{24,28},{28,0},{1,5},{5... | collective-permute-start | bytes 3145736 | tf_op jit(solution)/shard_map/ppermute | solution.py:68
  976.6 33.7 %collective-permute-start.28 = (f32[2,256,256]{2,1,0:T(8,128)}, f32[2,256,256]{2,1,0:T(8,128)}, u32[]{:S(2)}, u32[]{:S(2)}) collective-permute-start(f32[2,256,256]{2,1,0:T(8,128)} %pad_add_fusion.7.lt), channel_id=1, source_target_pairs={{0,28},{4,0},{8,4},{12,8},{16,12},{20,16},{24,20},{28,24},{1,29},{... | collective-permute-start | bytes 1572872 | tf_op jit(solution)/shard_map/ppermute | solution.py:68
  (37 other events, 719.4 us)
Sparse Core Ops, SparseCore 0:
  9.1 83.4 all-gather.4
  94.2 148.0 all-gather.2

commit v3 on v2

--- a/solution.py
+++ b/solution.py
@@ -130,6 +130,32 @@
     )(jnp.asarray(spots, jnp.int32).reshape(-1), matrix)
 
 
+def row_factors(g, scalars, source, prior):
+    W, half = g.win, g.half
+
+    def kernel(s, q1, qp, q2, bh, bl, th, tl, qh, ql):
+        bh[0], bl[0] = split(q1[0, 0].T[:half])
+        th[0], tl[0] = split(qp[0].T)
+        qh[0], ql[0] = split(q2[0, 0].T)
+
+    part = pl.BlockSpec((1, half, W), lambda i, s: (i, 0, 0))
+    size = g.kb * W * W
+    return call(
+        kernel,
+        g.kb,
+        [
+            pl.BlockSpec((1, 1, W, W), lambda i, s: (0, i, 0, 0)),
+            pl.BlockSpec((1, W, half), lambda i, s: (i, 0, 0)),
+            pl.BlockSpec((1, 1, W, W), lambda i, s: (1, i, 0, 0)),
+        ],
+        [part] * 4 + [pl.BlockSpec((1, W, W), lambda i, s: (i, 0, 0))] * 2,
+        [shape((g.kb, half, W), BF16)] * 4 + [shape((g.kb, W, W), BF16)] * 2,
+        [],
+        size,
+        20 * size,
+    )(scalars, source, prior, source)
+
+
 def even_first(g, k, scalars, matrix, row_factor, col_hi, col_lo):
     W, half, lo_m, n = g.win, g.half, g.first(k), g.count(k)
 
@@ -159,18 +185,14 @@
             left[0] = y[:, :half]
             right[0] = y[:, half:]
 
-            @pl.when(i > 0)
-            def _():
-                later[0] = y[:, :half]
-
         @pl.when(jnp.logical_not(do_right))
         def _():
             left[0] = x[:, :half]
             right[0] = x[:, half:]
 
-            @pl.when(i > 0)
-            def _():
-                later[0] = x[:, :half]
+        @pl.when(i > 0)
+        def _():
+            later[0] = left[0]
 
     return call(
         kernel,
@@ -255,7 +277,6 @@
 
 def finish(g, k, scalars, matrix, factors, col_hi, col_lo, own, below, above, out):
     W, half, lo_m, n = g.win, g.half, g.first(k), g.count(k)
-    later, prior = factors
 
     def spec(source, wanted=None):
         size, start = g.count(source), g.first(source)
@@ -272,22 +293,16 @@
     top_edge = lambda s: s[0] == 0
     has_next, has_prev = below[1] is not None, above[1] is not None
 
-    def kernel(s, h_ref, q1, qp, q2, ch, cl, lt, lb, rt, rb, *rest):
+    def kernel(s, h_ref, bh, bl, th, tl, qh, ql, ch, cl, lt, lb, rt, rb, *rest):
         rest = list(rest)
         take = lambda: (rest.pop(0), rest.pop(0))
         below_here, above_here = take(), take()
         below_next = take() if has_next else below_here
         above_prev = take() if has_prev else above_here
         rest.pop(0)
-        o_ref, bh, bl, th, tl, qh, ql, x = rest
+        o_ref, x = rest
         i = pl.program_id(0)
         r, c = k * g.R + s[0], (lo_m + i) * g.C + s[1]
-
-        @pl.when(i == 0)
-        def _():
-            bh[...], bl[...] = split(q1[0, 0].T[:half])
-            th[...], tl[...] = split(qp[0].T)
-            qh[...], ql[...] = split(q2[0, 0].T)
 
         @pl.when(c < r)
         def _():
@@ -312,14 +327,14 @@
             def _():
                 upper = chosen(above_here, above_prev, top_edge(s), has_prev)
                 lower = jnp.concatenate([lt[0], rt[0]], axis=1)
-                y = mul((th[...], tl[...]), split(jnp.concatenate([upper, lower], axis=0)))
+                y = mul((th[0], tl[0]), split(jnp.concatenate([upper, lower], axis=0)))
                 x[:half, :] = y
 
             @pl.when(do_bottom)
             def _():
                 upper = jnp.concatenate([lb[0], rb[0]], axis=1)
                 lower = chosen(below_here, below_next, bottom_edge(s), has_next)
-                y = mul((bh[...], bl[...]), split(jnp.concatenate([upper, lower], axis=0)))
+                y = mul((bh[0], bl[0]), split(jnp.concatenate([upper, lower], axis=0)))
                 x[half:, half:] = y[:, half:]
 
                 @pl.when(c > r + 1)
@@ -332,7 +347,7 @@
 
             @pl.when((c > r) & flag(s, g, 2, r))
             def _():
-                x[...] = mul((qh[...], ql[...]), split(x[...]))
+                x[...] = mul((qh[0], ql[0]), split(x[...]))
 
             do_right = (c > r) & flag(s, g, 2, c)
 
@@ -345,15 +360,18 @@
                 o_ref[...] = x[...]
 
     column = pl.BlockSpec((1, W, W), lambda i, s: (lo_m + i, 0, 0))
-    operands = [matrix, later, prior, later, col_hi, col_lo, *own, *below[0], *above[0]]
+    operands = [matrix, *factors, col_hi, col_lo, *own, *below[0], *above[0]]
     in_specs = [
         pl.BlockSpec((W, W), lambda i, s: (k, lo_m + i)),
-        pl.BlockSpec((1, 1, W, W), lambda i, s: (0, k, 0, 0)),
-        pl.BlockSpec(
-            (1, W, half),
-            lambda i, s: (jnp.maximum(k - jnp.where(s[0] == 0, 1, 0), 0), 0, 0),
-        ),
-        pl.BlockSpec((1, 1, W, W), lambda i, s: (1, k, 0, 0)),
+        *[pl.BlockSpec((1, half, W), lambda i, s: (k, 0, 0))] * 2,
+        *[
+            pl.BlockSpec(
+                (1, half, W),
+                lambda i, s: (jnp.maximum(k - jnp.where(s[0] == 0, 1, 0), 0), 0, 0),
+            )
+        ]
+        * 2,
+        *[pl.BlockSpec((1, W, W), lambda i, s: (k, 0, 0))] * 2,
         column,
         column,
         spec(k),
@@ -380,9 +398,7 @@
         in_specs,
         pl.BlockSpec((W, W), lambda i, s: (k, lo_m + i)),
         shape(matrix.shape),
-        [pltpu.VMEM((half, W), BF16)] * 4
-        + [pltpu.VMEM((W, W), BF16)] * 2
-        + [pltpu.VMEM((W, W), F32)],
+        [pltpu.VMEM((W, W), F32)],
         18 * n * W**3,
         24 * n * W * W,
         aliases,
@@ -434,6 +450,8 @@
 
     col_factor = [columns(first, 0), columns(odd_last, 0)]
     prior = ring(odd_last[0, :, :, g.half :], "row", 1)
+
+    finish_factors = row_factors(g, scalars, odd_last, prior)
 
     own, tops, bottoms = [], [], []
     for k in range(g.kb):
@@ -468,7 +486,7 @@
             k,
             scalars,
             hessenberg,
-            (odd_last, prior),
+            finish_factors,
             *col_factor[2],
             own[k],
             below,

time: 1060 us -> 1050 us (level)
  transfers between devices with their start and end apart: 64 -> 64, of which waited for: 32 -> 32; matrix products, arithmetic and copies ran while one was open for 5% -> 4% of each run, Pallas kernels for 18% -> 18%
where the time goes in v3:
time: 1050 us
  waiting for transfers between devices  681 us (65%)
  Pallas kernels  202 us (19%)
  starting transfers between devices  97.7 us (9%)
  other arithmetic  33.2 us (3%)
  local copies, waits for them, and re-layouts  22.1 us (2%)
  between operations  14.1 us (1%)
    ppermute x12, waiting for transfers between devices, around(): return lax.ppermute(value, axis, [(last, 0) if steps > 0 else (0, last)])  213 us
    ppermute x12, waiting for transfers between devices, along(): return lax.ppermute(value, axis, pairs)  105 us
    all_gather x1, waiting for transfers between devices, local(): first = lax.all_gather(factors[:1], 'col', axis=2, tiled=True)  81.9 us
    ppermute x17, waiting for transfers between devices, ring(): lax.ppermute(value, axis, [(s, (s + steps) % size) for s in range(size)])  76.9 us
    all_gather x1, waiting for transfers between devices, local(): odd_last = lax.all_gather(factors[1:], 'col', axis=2, tiled=True)  71.2 us
    ppermute x9, waiting for transfers between devices, columns(): piece = piece + lax.ppermute(cut[d], ('row', 'col'), spread[d])  69 us
    pallas_call x4, Pallas kernels, finish(): call(kernel, n, in_specs, pl.BlockSpec((W, W), lambda i, s: (k, lo_m + i)...  65.9 us
    ppermute x12, waiting for transfers between devices, swap(): return lax.ppermute(value, axis, [(s, s ^ bit) for s in range(size)])  64.4 us
  transfers between devices with their start and end apart: 64, of which 32 were waited for; matrix products, arithmetic and copies ran while one was open for 4% of the time, Pallas kernels for 18%

profile of v3, /device:TPU:0, one launch (start us, length us, event | category | flops | bytes accessed | tf_op | source)
XLA Modules:
  0.0 1050.2 jit_solution(9261257873069681697)
XLA Ops:
  10.7 81.9 %all-gather.5.cloned.1.call-done.q_ref = f32[1,4,512,512]{3,2,1,0:T(8,128)} async-done(((f32[1,4,128,512]{3,2,1,0:T(8,128)}), f32[1,4,512,512]{3,2,1,0:T(8,128)}) %all-gather.5.cloned.1.call-update) | async-done | bytes 4194320 | tf_op jit(solution)/shard_map/all_gather | solution.py:429
  102.0 10.2 collective-permute-done.10
  112.2 16.5 %collective-permute-done.9 = f32[4,128,512]{2,1,0:T(8,128)} collective-permute-done((f32[4,128,512]{2,1,0:T(8,128)S(1)}, f32[4,128,512]{2,1,0:T(8,128)}, u32[]{:S(2)}, u32[]{:S(2)}) %collective-permute-start.9) | collective-permute-done | bytes 1048608 | tf_op jit(solution)/shard_map/ppermute | solution.py:443
  136.0 21.2 %collective-permute-done.13 = f32[4,128,512]{2,1,0:T(8,128)S(1)} collective-permute-done((f32[4,128,512]{2,1,0:T(8,128)S(1)}, f32[4,128,512]{2,1,0:T(8,128)S(1)}, u32[]{:S(2)}, u32[]{:S(2)}) %collective-permute-start.13) | collective-permute-done | bytes 1048608 | tf_op jit(solution)/shard_map/ppermute | solution.py:84
  157.2 6.5 collective-permute-done.12
  171.1 71.2 %all-gather.3.cloned.1.call-done.q1.q2 = f32[2,4,512,512]{3,2,1,0:T(8,128)} async-done(((f32[2,4,128,512]{3,2,1,0:T(8,128)}), f32[2,4,512,512]{3,2,1,0:T(8,128)}) %all-gather.3.cloned.1.call-update) | async-done | bytes 8388624 | tf_op jit(solution)/shard_map/all_gather | solution.py:430
  242.3 5.8 dynamic-slice_bitcast_fusion.2
  256.9 7.2 collective-permute-done.19
  268.9 11.2 %collective-permute-done.18 = f32[4,128,512]{2,1,0:T(8,128)S(1)} collective-permute-done((f32[4,128,512]{2,1,0:T(8,128)S(1)}, f32[4,128,512]{2,1,0:T(8,128)S(1)}, u32[]{:S(2)}, u32[]{:S(2)}) %collective-permute-start.18) | collective-permute-done | bytes 1048608 | tf_op jit(solution)/shard_map/ppermute | solution.py:443
  287.6 8.0 shard_map.48
  295.6 7.1 collective-permute-done.2
  303.7 16.7 %collective-permute-done.3 = f32[4,128,512]{2,1,0:T(8,128)} collective-permute-done((f32[4,128,512]{2,1,0:T(8,128)}, f32[4,128,512]{2,1,0:T(8,128)}, u32[]{:S(2)}, u32[]{:S(2)}) %collective-permute-start.3) | collective-permute-done | bytes 1048608 | tf_op jit(solution)/shard_map/ppermute | solution.py:443
  322.8 13.8 %collective-permute-done.22 = f32[4,128,512]{2,1,0:T(8,128)} collective-permute-done((f32[4,128,512]{2,1,0:T(8,128)S(1)}, f32[4,128,512]{2,1,0:T(8,128)}, u32[]{:S(2)}, u32[]{:S(2)}) %collective-permute-start.22) | collective-permute-done | bytes 1048608 | tf_op jit(solution)/shard_map/ppermute | solution.py:84
  336.6 17.4 %collective-permute-done.20 = f32[4,128,512]{2,1,0:T(8,128)} collective-permute-done((f32[4,128,512]{2,1,0:T(8,128)S(1)}, f32[4,128,512]{2,1,0:T(8,128)}, u32[]{:S(2)}, u32[]{:S(2)}) %collective-permute-start.20) | collective-permute-done | bytes 1048608 | tf_op jit(solution)/shard_map/ppermute | solution.py:84
  358.5 6.4 shard_map.49
  369.1 10.5 %shard_map.52 = (f32[4,512,256]{2,1,0:T(8,128)}, f32[3,512,256]{2,1,0:T(8,128)}, f32[4,512,256]{2,1,0:T(8,128)}) custom-call(s32[98]{0:T(128)} %pad_add_fusion.8.s, f32[2048,4096]{1,0:T(8,128)} %h_ref.17, f32[1,4,512,512]{3,2,1,0:T(8,128)} %all-gather.5.cloned.1.call-done.q_ref, bf16[8,512,512]{2,1,0:T(8,128)(2,1)} %get-tuple-element.69.ch, ...), custom_call_target="tpu_custom_call" | custom-call | flops 6442450944 | bytes 12582912 | tf_op jit(solution)/shard_map/pallas_call | solution.py:197
  382.9 8.6 collective-permute-start.33
  395.4 18.0 %shard_map.56 = (f32[8,512,256]{2,1,0:T(8,128)}, f32[7,512,256]{2,1,0:T(8,128)}, f32[8,512,256]{2,1,0:T(8,128)}) custom-call(s32[98]{0:T(128)} %pad_add_fusion.8.s, f32[2048,4096]{1,0:T(8,128)} %h_ref.17, f32[1,4,512,512]{3,2,1,0:T(8,128)} %all-gather.5.cloned.1.call-done.q_ref, bf16[8,512,512]{2,1,0:T(8,128)(2,1)} %get-tuple-element.69.ch, ...), custom_call_target="tpu_custom_call" | custom-call | flops 12884901888 | bytes 25165824 | tf_op jit(solution)/shard_map/pallas_call | solution.py:197
  418.0 33.9 %collective-permute-done.15.b_ref = f32[2,512,256]{2,1,0:T(8,128)} collective-permute-done((f32[2,512,256]{2,1,0:T(8,128)}, f32[2,512,256]{2,1,0:T(8,128)}, u32[]{:S(2)}, u32[]{:S(2)}) %collective-permute-start.15) | collective-permute-done | bytes 1048608 | tf_op jit(solution)/shard_map/ppermute | solution.py:74
  451.9 5.0 collective-permute-start.53
  458.3 12.4 %shard_map.54 = (f32[6,512,256]{2,1,0:T(8,128)}, f32[5,512,256]{2,1,0:T(8,128)}, f32[6,512,256]{2,1,0:T(8,128)}) custom-call(s32[98]{0:T(128)} %pad_add_fusion.8.s, f32[2048,4096]{1,0:T(8,128)} %h_ref.17, f32[1,4,512,512]{3,2,1,0:T(8,128)} %all-gather.5.cloned.1.call-done.q_ref, bf16[8,512,512]{2,1,0:T(8,128)(2,1)} %get-tuple-element.69.ch, ...), custom_call_target="tpu_custom_call" | custom-call | flops 9663676416 | bytes 18874368 | tf_op jit(solution)/shard_map/pallas_call | solution.py:197
  472.0 8.2 collective-permute-start.43
  480.3 8.1 shard_map.50
  488.4 5.7 shard_map.51
  494.0 95.0 %collective-permute-done.43.e_ref = f32[5,512,256]{2,1,0:T(8,128)S(1)} collective-permute-done((f32[5,512,256]{2,1,0:T(8,128)}, f32[5,512,256]{2,1,0:T(8,128)S(1)}, u32[]{:S(2)}, u32[]{:S(2)}) %collective-permute-start.43) | collective-permute-done | bytes 2621472 | tf_op jit(solution)/shard_map/ppermute | solution.py:79
  591.8 25.5 %collective-permute-done.42.b_ref = f32[6,512,256]{2,1,0:T(8,128)} collective-permute-done((f32[6,512,256]{2,1,0:T(8,128)}, f32[6,512,256]{2,1,0:T(8,128)}, u32[]{:S(2)}, u32[]{:S(2)}) %collective-permute-start.42) | collective-permute-done | bytes 3145760 | tf_op jit(solution)/shard_map/ppermute | solution.py:74
  618.8 9.1 shard_map.53
  631.9 12.4 %shard_map.55 = (f32[6,256,256]{2,1,0:T(8,128)}, f32[6,256,256]{2,1,0:T(8,128)}, f32[5,256,256]{2,1,0:T(8,128)}, f32[5,256,256]{2,1,0:T(8,128)}, f32[6,256,256]{2,1,0:T(8,128)}, /*index=5*/f32[6,256,256]{2,1,0:T(8,128)}) custom-call(s32[98]{0:T(128)} %pad_add_fusion.8.s, f32[6,512,256]{2,1,0:T(8,128)} %get-tuple-element.91.r_ref, ...), custom_call_target="tpu_custom_call" | custom-call | flops 4831838208 | bytes 18874368 | tf_op jit(solution)/shard_map/pallas_call | solution.py:257
  653.4 14.8 %shard_map.57 = (f32[8,256,256]{2,1,0:T(8,128)}, f32[8,256,256]{2,1,0:T(8,128)}, f32[7,256,256]{2,1,0:T(8,128)}, f32[7,256,256]{2,1,0:T(8,128)}, f32[8,256,256]{2,1,0:T(8,128)}, /*index=5*/f32[8,256,256]{2,1,0:T(8,128)}) custom-call(s32[98]{0:T(128)} %pad_add_fusion.8.s, f32[8,512,256]{2,1,0:T(8,128)} %get-tuple-element.100.r_ref, ...), custom_call_target="tpu_custom_call" | custom-call | flops 6442450944 | bytes 25165824 | tf_op jit(solution)/shard_map/pallas_call | solution.py:257
  669.5 10.7 %collective-permute-done.39 = f32[3,256,256]{2,1,0:T(8,128)} collective-permute-done((f32[3,256,256]{2,1,0:T(8,128)}, f32[3,256,256]{2,1,0:T(8,128)}, u32[]{:S(2)}, u32[]{:S(2)}) %collective-permute-start.39) | collective-permute-done | bytes 786464 | tf_op jit(solution)/shard_map/ppermute | solution.py:79
  683.0 11.8 %collective-permute-done.38 = f32[4,256,256]{2,1,0:T(8,128)S(1)} collective-permute-done((f32[4,256,256]{2,1,0:T(8,128)}, f32[4,256,256]{2,1,0:T(8,128)S(1)}, u32[]{:S(2)}, u32[]{:S(2)}) %collective-permute-start.38) | collective-permute-done | bytes 1048608 | tf_op jit(solution)/shard_map/ppermute | solution.py:74
  699.2 9.1 collective-permute-done.45
  709.6 66.1 %collective-permute-done.49 = f32[5,256,256]{2,1,0:T(8,128)S(1)} collective-permute-done((f32[5,256,256]{2,1,0:T(8,128)}, f32[5,256,256]{2,1,0:T(8,128)S(1)}, u32[]{:S(2)}, u32[]{:S(2)}) %collective-permute-start.49) | collective-permute-done | bytes 1310752 | tf_op jit(solution)/shard_map/ppermute | solution.py:79
  780.3 30.4 %collective-permute-done.59 = f32[7,256,256]{2,1,0:T(8,128)S(1)} collective-permute-done((f32[7,256,256]{2,1,0:T(8,128)}, f32[7,256,256]{2,1,0:T(8,128)S(1)}, u32[]{:S(2)}, u32[]{:S(2)}) %collective-permute-start.59) | collective-permute-done | bytes 1835040 | tf_op jit(solution)/shard_map/ppermute | solution.py:79
  818.4 30.2 %collective-permute-done.48 = f32[6,256,256]{2,1,0:T(8,128)S(1)} collective-permute-done((f32[6,256,256]{2,1,0:T(8,128)}, f32[6,256,256]{2,1,0:T(8,128)S(1)}, u32[]{:S(2)}, u32[]{:S(2)}) %collective-permute-start.48) | collective-permute-done | bytes 1572896 | tf_op jit(solution)/shard_map/ppermute | solution.py:74
  851.0 13.9 %shard_map.58.rest_6_ = f32[2048,4096]{1,0:T(8,128)} custom-call(s32[24]{0:T(128)} %constant.91.s, f32[2048,4096]{1,0:T(8,128)} %h_ref.17), custom_call_target="tpu_custom_call" | custom-call | flops 3145728 | bytes 25165824 | tf_op jit(solution)/shard_map/pallas_call | solution.py:128
  864.9 8.3 shard_map.46
  873.2 8.1 shard_map.47
  891.5 30.0 %collective-permute-done.50.rest_4_.rest_0_ = f32[6,256,256]{2,1,0:T(8,128)} collective-permute-done((f32[6,256,256]{2,1,0:T(8,128)}, f32[6,256,256]{2,1,0:T(8,128)}, u32[]{:S(2)}, u32[]{:S(2)}) %collective-permute-start.50) | collective-permute-done | bytes 1572896 | tf_op jit(solution)/shard_map/ppermute | solution.py:68
  924.3 22.3 %shard_map.59.rest_8_ = f32[2048,4096]{1,0:T(8,128)} custom-call(s32[98]{0:T(128)} %pad_add_fusion.8.s, f32[2048,4096]{1,0:T(8,128)} %h_ref.17, bf16[4,256,512]{2,1,0:T(8,128)(2,1)} %get-tuple-element.57.bh, bf16[4,256,512]{2,1,0:T(8,128)(2,1)} %get-tuple-element.58.bl, bf16[4,256,512]{2,1,0:T(8,128)(2,1)} %get-tuple-element.59.th, ...), custom_call_target="tpu_custom_call", output_to_operand_aliasing={{}: (20, {})} | custom-call | flops 19327352832 | bytes 50331648 | tf_op jit(solution)/shard_map/pallas_call | solution.py:395
  946.6 7.8 collective-permute-done.41.rest_5_.rest_1_
  954.4 5.1 collective-permute-done.47.rest_3_.rest_7_
  959.6 17.3 %collective-permute-done.40.rest_4_.rest_0_ = f32[4,256,256]{2,1,0:T(8,128)} collective-permute-done((f32[4,256,256]{2,1,0:T(8,128)}, f32[4,256,256]{2,1,0:T(8,128)}, u32[]{:S(2)}, u32[]{:S(2)}) %collective-permute-start.40) | collective-permute-done | bytes 1048608 | tf_op jit(solution)/shard_map/ppermute | solution.py:68
  979.7 9.4 collective-permute-done.46.rest_2_.rest_6_
  989.1 19.1 %shard_map.60.rest_8_ = f32[2048,4096]{1,0:T(8,128)} custom-call(s32[98]{0:T(128)} %pad_add_fusion.8.s, f32[2048,4096]{1,0:T(8,128)} %h_ref.17, bf16[4,256,512]{2,1,0:T(8,128)(2,1)} %get-tuple-element.57.bh, bf16[4,256,512]{2,1,0:T(8,128)(2,1)} %get-tuple-element.58.bl, bf16[4,256,512]{2,1,0:T(8,128)(2,1)} %get-tuple-element.59.th, ...), custom_call_target="tpu_custom_call", output_to_operand_aliasing={{}: (22, {})} | custom-call | flops 14495514624 | bytes 37748736 | tf_op jit(solution)/shard_map/pallas_call | solution.py:395
  1009.9 7.2 collective-permute-done.36.rest_2_.rest_4_
  1018.0 15.3 %shard_map.61.rest_6_ = f32[2048,4096]{1,0:T(8,128)} custom-call(s32[98]{0:T(128)} %pad_add_fusion.8.s, f32[2048,4096]{1,0:T(8,128)} %h_ref.17, bf16[4,256,512]{2,1,0:T(8,128)(2,1)} %get-tuple-element.57.bh, bf16[4,256,512]{2,1,0:T(8,128)(2,1)} %get-tuple-element.58.bl, bf16[4,256,512]{2,1,0:T(8,128)(2,1)} %get-tuple-element.59.th, ...), custom_call_target="tpu_custom_call", output_to_operand_aliasing={{}: (22, {})} | custom-call | flops 9663676416 | bytes 25165824 | tf_op jit(solution)/shard_map/pallas_call | solution.py:395
  1034.1 9.2 shard_map.62
  (166 shorter events, 136.2 us)
Async XLA Ops:
  6.5 86.1 %all-gather.5.cloned.1.call-start = ((), (), s32[]{:S(2)}) async-start(), calls=%async_computation.1 | async-start | bytes 5242880 | tf_op jit(solution)/shard_map/all_gather | solution.py:429
  9.0 233.3 %all-gather.3.cloned.1.call-start = ((), (), s32[]{:S(2)}) async-start(), calls=%async_computation | async-start | bytes 10485760 | tf_op jit(solution)/shard_map/all_gather | solution.py:430
  135.3 33.1 %collective-permute-start.11 = (f32[4,128,512]{2,1,0:T(8,128)S(1)}, f32[4,128,512]{2,1,0:T(8,128)S(1)}, u32[]{:S(2)}, u32[]{:S(2)}) collective-permute-start(f32[4,128,512]{2,1,0:T(8,128)S(1)} %fusion.3), channel_id=1, source_target_pairs={{0,8},{4,12},{8,0},{12,4},{16,24},{20,28},{24,16},{28,20},{1,9},{5... | collective-permute-start | bytes 3145736 | tf_op jit(solution)/shard_map/ppermute | solution.py:84
  171.1 115.2 %collective-permute-start.14 = (f32[4,4,128,512]{3,2,1,0:T(8,128)}, f32[4,4,128,512]{3,2,1,0:T(8,128)}, u32[]{:S(2)}, u32[]{:S(2)}) collective-permute-start(f32[4,4,128,512]{3,2,1,0:T(8,128)} %pad_maximum_fusion.1.same_ref), channel_id=1, source_target_pairs={{0,4},{4,0},{8,12},{12,8},{16,20},{20,16},{24,28},{28,24},{1,5},{5... | collective-permute-start | bytes 12582920 | tf_op jit(solution)/shard_map/ppermute | solution.py:84
  253.3 33.0 %collective-permute-start.1 = (f32[4,128,512]{2,1,0:T(8,128)S(1)}, f32[4,128,512]{2,1,0:T(8,128)}, u32[]{:S(2)}, u32[]{:S(2)}) collective-permute-start(f32[4,128,512]{2,1,0:T(8,128)S(1)} %get-tuple-element.64), channel_id=1, source_target_pairs={{0,4},{5,9},{10,14},{15,3},{16,20},{21,25},{26,30},{31,19}} | collective-permute-start | bytes 3145736 | tf_op jit(solution)/shard_map/ppermute | solution.py:443
  255.6 47.2 %collective-permute-start.2 = (f32[4,128,512]{2,1,0:T(8,128)}, f32[4,128,512]{2,1,0:T(8,128)S(1)}, u32[]{:S(2)}, u32[]{:S(2)}) collective-permute-start(f32[4,128,512]{2,1,0:T(8,128)} %get-tuple-element.65), channel_id=1, source_target_pairs={{0,8},{5,13},{10,2},{15,7},{16,24},{21,29},{26,18},{31,23}} | collective-permute-start | bytes 3145736 | tf_op jit(solution)/shard_map/ppermute | solution.py:443
  264.1 56.3 %collective-permute-start.3 = (f32[4,128,512]{2,1,0:T(8,128)}, f32[4,128,512]{2,1,0:T(8,128)}, u32[]{:S(2)}, u32[]{:S(2)}) collective-permute-start(f32[4,128,512]{2,1,0:T(8,128)} %get-tuple-element.66), channel_id=1, source_target_pairs={{0,12},{5,1},{10,6},{15,11},{16,28},{21,17},{26,22},{31,27}} | collective-permute-start | bytes 3145736 | tf_op jit(solution)/shard_map/ppermute | solution.py:443
  281.9 54.7 %collective-permute-start.22 = (f32[4,128,512]{2,1,0:T(8,128)S(1)}, f32[4,128,512]{2,1,0:T(8,128)}, u32[]{:S(2)}, u32[]{:S(2)}) collective-permute-start(f32[4,128,512]{2,1,0:T(8,128)S(1)} %fusion.1), channel_id=1, source_target_pairs={{0,24},{4,28},{8,16},{12,20},{16,8},{20,12},{24,0},{28,4},{1,25},{... | collective-permute-start | bytes 3145736 | tf_op jit(solution)/shard_map/ppermute | solution.py:84
  286.3 50.4 %collective-permute-start.21 = (f32[4,128,512]{2,1,0:T(8,128)S(1)}, f32[4,128,512]{2,1,0:T(8,128)}, u32[]{:S(2)}, u32[]{:S(2)}) collective-permute-start(f32[4,128,512]{2,1,0:T(8,128)S(1)} %fusion.1), channel_id=1, source_target_pairs={{0,16},{4,20},{8,24},{12,28},{16,0},{20,4},{24,8},{28,12},{1,17},{... | collective-permute-start | bytes 3145736 | tf_op jit(solution)/shard_map/ppermute | solution.py:84
  286.3 67.7 %collective-permute-start.20 = (f32[4,128,512]{2,1,0:T(8,128)S(1)}, f32[4,128,512]{2,1,0:T(8,128)}, u32[]{:S(2)}, u32[]{:S(2)}) collective-permute-start(f32[4,128,512]{2,1,0:T(8,128)S(1)} %fusion.1), channel_id=1, source_target_pairs={{0,8},{4,12},{8,0},{12,4},{16,24},{20,28},{24,16},{28,20},{1,9},{5... | collective-permute-start | bytes 3145736 | tf_op jit(solution)/shard_map/ppermute | solution.py:84
  322.8 59.1 %collective-permute-start.6 = (f32[4,128,512]{2,1,0:T(8,128)S(1)}, f32[4,128,512]{2,1,0:T(8,128)S(1)}, u32[]{:S(2)}, u32[]{:S(2)}) collective-permute-start(f32[4,128,512]{2,1,0:T(8,128)S(1)} %add_add_fusion), channel_id=1, source_target_pairs={{0,24},{4,28},{8,16},{12,20},{16,8},{20,12},{24,0},{28,4},{1,25},{... | collective-permute-start | bytes 3145736 | tf_op jit(solution)/shard_map/ppermute | solution.py:84
  358.5 113.6 %collective-permute-start.23 = (f32[4,4,128,512]{3,2,1,0:T(8,128)}, f32[4,4,128,512]{3,2,1,0:T(8,128)}, u32[]{:S(2)}, u32[]{:S(2)}) collective-permute-start(f32[4,4,128,512]{3,2,1,0:T(8,128)} %pad_maximum_fusion.2.same_ref), channel_id=1, source_target_pairs={{0,4},{4,0},{8,12},{12,8},{16,20},{20,16},{24,28},{28,24},{1,5},{5... | collective-permute-start | bytes 12582920 | tf_op jit(solution)/shard_map/ppermute | solution.py:84
  380.6 77.7 %collective-permute-start.32 = (f32[4,512,256]{2,1,0:T(8,128)}, f32[4,512,256]{2,1,0:T(8,128)}, u32[]{:S(2)}, u32[]{:S(2)}) collective-permute-start(f32[4,512,256]{2,1,0:T(8,128)} %get-tuple-element.83), channel_id=1, source_target_pairs={{1,0},{2,1},{3,2},{5,4},{6,5},{7,6},{9,8},{10,9},{11,10},{13,12},{... | collective-permute-start | bytes 6291464 | tf_op jit(solution)/shard_map/ppermute | solution.py:74
  382.9 74.1 %collective-permute-start.33 = (f32[3,512,256]{2,1,0:T(8,128)}, f32[3,512,256]{2,1,0:T(8,128)}, u32[]{:S(2)}, u32[]{:S(2)}) collective-permute-start(f32[3,512,256]{2,1,0:T(8,128)} %get-tuple-element.84), channel_id=1, source_target_pairs={{0,3},{4,7},{8,11},{12,15},{16,19},{20,23},{24,27},{28,31}} | collective-permute-start | bytes 4718600 | tf_op jit(solution)/shard_map/ppermute | solution.py:79
  393.9 58.0 %collective-permute-start.15 = (f32[2,512,256]{2,1,0:T(8,128)}, f32[2,512,256]{2,1,0:T(8,128)}, u32[]{:S(2)}, u32[]{:S(2)}) collective-permute-start(f32[2,512,256]{2,1,0:T(8,128)} %get-tuple-element.72), channel_id=1, source_target_pairs={{1,0},{2,1},{3,2},{5,4},{6,5},{7,6},{9,8},{10,9},{11,10},{13,12},{... | collective-permute-start | bytes 3145736 | tf_op jit(solution)/shard_map/ppermute | solution.py:74
  395.2 75.5 %collective-permute-start = (f32[4,512,256]{2,1,0:T(8,128)S(1)}, f32[4,512,256]{2,1,0:T(8,128)}, u32[]{:S(2)}, u32[]{:S(2)}) collective-permute-start(f32[4,512,256]{2,1,0:T(8,128)S(1)} %slice_bitcast_fusion), channel_id=1, source_target_pairs={{0,4},{4,8},{8,12},{12,16},{16,20},{20,24},{24,28},{28,0},{1,5},{5... | collective-permute-start | bytes 6291464 | tf_op jit(solution)/shard_map/ppermute | solution.py:68
  451.9 176.1 %collective-permute-start.53 = (f32[7,512,256]{2,1,0:T(8,128)}, f32[7,512,256]{2,1,0:T(8,128)}, u32[]{:S(2)}, u32[]{:S(2)}) collective-permute-start(f32[7,512,256]{2,1,0:T(8,128)} %get-tuple-element.102), channel_id=1, source_target_pairs={{0,3},{4,7},{8,11},{12,15},{16,19},{20,23},{24,27},{28,31}} | collective-permute-start | bytes 11010056 | tf_op jit(solution)/shard_map/ppermute | solution.py:79
  456.9 172.3 %collective-permute-start.52 = (f32[8,512,256]{2,1,0:T(8,128)}, f32[8,512,256]{2,1,0:T(8,128)}, u32[]{:S(2)}, u32[]{:S(2)}) collective-permute-start(f32[8,512,256]{2,1,0:T(8,128)} %get-tuple-element.101), channel_id=1, source_target_pairs={{1,0},{2,1},{3,2},{5,4},{6,5},{7,6},{9,8},{10,9},{11,10},{13,12},{... | collective-permute-start | bytes 12582920 | tf_op jit(solution)/shard_map/ppermute | solution.py:74
  458.2 172.4 %collective-permute-start.7 = (f32[4,4,128,512]{3,2,1,0:T(8,128)}, f32[4,4,128,512]{3,2,1,0:T(8,128)}, u32[]{:S(2)}, u32[]{:S(2)}) collective-permute-start(f32[4,4,128,512]{3,2,1,0:T(8,128)} %pad_maximum_fusion.same_ref), channel_id=1, source_target_pairs={{0,4},{4,0},{8,12},{12,8},{16,20},{20,16},{24,28},{28,24},{1,5},{5... | collective-permute-start | bytes 12582920 | tf_op jit(solution)/shard_map/ppermute | solution.py:84
  470.7 146.6 %collective-permute-start.42 = (f32[6,512,256]{2,1,0:T(8,128)}, f32[6,512,256]{2,1,0:T(8,128)}, u32[]{:S(2)}, u32[]{:S(2)}) collective-permute-start(f32[6,512,256]{2,1,0:T(8,128)} %get-tuple-element.92), channel_id=1, source_target_pairs={{1,0},{2,1},{3,2},{5,4},{6,5},{7,6},{9,8},{10,9},{11,10},{13,12},{... | collective-permute-start | bytes 9437192 | tf_op jit(solution)/shard_map/ppermute | solution.py:74
  472.0 117.0 %collective-permute-start.43 = (f32[5,512,256]{2,1,0:T(8,128)}, f32[5,512,256]{2,1,0:T(8,128)S(1)}, u32[]{:S(2)}, u32[]{:S(2)}) collective-permute-start(f32[5,512,256]{2,1,0:T(8,128)} %get-tuple-element.93), channel_id=1, source_target_pairs={{0,3},{4,7},{8,11},{12,15},{16,19},{20,23},{24,27},{28,31}} | collective-permute-start | bytes 7864328 | tf_op jit(solution)/shard_map/ppermute | solution.py:79
  590.5 58.0 %collective-permute-start.24 = (f32[2,256,256]{2,1,0:T(8,128)}, f32[2,256,256]{2,1,0:T(8,128)S(1)}, u32[]{:S(2)}, u32[]{:S(2)}) collective-permute-start(f32[2,256,256]{2,1,0:T(8,128)} %get-tuple-element.76), channel_id=1, source_target_pairs={{0,1},{1,2},{2,3},{4,5},{5,6},{6,7},{8,9},{9,10},{10,11},{12,13},{... | collective-permute-start | bytes 1572872 | tf_op jit(solution)/shard_map/ppermute | solution.py:74
  617.3 34.0 %collective-permute-start.26 = (f32[2,256,256]{2,1,0:T(8,128)}, f32[2,256,256]{2,1,0:T(8,128)S(1)}, u32[]{:S(2)}, u32[]{:S(2)}) collective-permute-start(f32[2,256,256]{2,1,0:T(8,128)} %get-tuple-element.78), channel_id=1, source_target_pairs={{0,1},{1,2},{2,3},{4,5},{5,6},{6,7},{8,9},{9,10},{10,11},{12,13},{... | collective-permute-start | bytes 1572872 | tf_op jit(solution)/shard_map/ppermute | solution.py:74
  630.6 37.6 %collective-permute-start.35 = (f32[3,256,256]{2,1,0:T(8,128)}, f32[3,256,256]{2,1,0:T(8,128)}, u32[]{:S(2)}, u32[]{:S(2)}) collective-permute-start(f32[3,256,256]{2,1,0:T(8,128)} %get-tuple-element.86), channel_id=1, source_target_pairs={{3,0},{7,4},{11,8},{15,12},{19,16},{23,20},{27,24},{31,28}} | collective-permute-start | bytes 2359304 | tf_op jit(solution)/shard_map/ppermute | solution.py:79
  644.3 36.0 %collective-permute-start.39 = (f32[3,256,256]{2,1,0:T(8,128)}, f32[3,256,256]{2,1,0:T(8,128)}, u32[]{:S(2)}, u32[]{:S(2)}) collective-permute-start(f32[3,256,256]{2,1,0:T(8,128)} %get-tuple-element.89), channel_id=1, source_target_pairs={{3,0},{7,4},{11,8},{15,12},{19,16},{23,20},{27,24},{31,28}} | collective-permute-start | bytes 2359304 | tf_op jit(solution)/shard_map/ppermute | solution.py:79
  646.5 35.2 %collective-permute-start.34 = (f32[4,256,256]{2,1,0:T(8,128)}, f32[4,256,256]{2,1,0:T(8,128)S(1)}, u32[]{:S(2)}, u32[]{:S(2)}) collective-permute-start(f32[4,256,256]{2,1,0:T(8,128)} %get-tuple-element.85), channel_id=1, source_target_pairs={{0,1},{1,2},{2,3},{4,5},{5,6},{6,7},{8,9},{9,10},{10,11},{12,13},{... | collective-permute-start | bytes 3145736 | tf_op jit(solution)/shard_map/ppermute | solution.py:74
  649.4 45.4 %collective-permute-start.38 = (f32[4,256,256]{2,1,0:T(8,128)}, f32[4,256,256]{2,1,0:T(8,128)S(1)}, u32[]{:S(2)}, u32[]{:S(2)}) collective-permute-start(f32[4,256,256]{2,1,0:T(8,128)} %get-tuple-element.88), channel_id=1, source_target_pairs={{0,1},{1,2},{2,3},{4,5},{5,6},{6,7},{8,9},{9,10},{10,11},{12,13},{... | collective-permute-start | bytes 3145736 | tf_op jit(solution)/shard_map/ppermute | solution.py:74
  652.1 56.2 %collective-permute-start.45 = (f32[5,256,256]{2,1,0:T(8,128)}, f32[5,256,256]{2,1,0:T(8,128)S(1)}, u32[]{:S(2)}, u32[]{:S(2)}) collective-permute-start(f32[5,256,256]{2,1,0:T(8,128)} %get-tuple-element.95), channel_id=1, source_target_pairs={{3,0},{7,4},{11,8},{15,12},{19,16},{23,20},{27,24},{31,28}} | collective-permute-start | bytes 3932168 | tf_op jit(solution)/shard_map/ppermute | solution.py:79
  668.2 108.8 %collective-permute-start.55 = (f32[7,256,256]{2,1,0:T(8,128)}, f32[7,256,256]{2,1,0:T(8,128)S(1)}, u32[]{:S(2)}, u32[]{:S(2)}) collective-permute-start(f32[7,256,256]{2,1,0:T(8,128)} %get-tuple-element.104), channel_id=1, source_target_pairs={{3,0},{7,4},{11,8},{15,12},{19,16},{23,20},{27,24},{31,28}} | collective-permute-start | bytes 5505032 | tf_op jit(solution)/shard_map/ppermute | solution.py:79
  680.3 98.2 %collective-permute-start.54 = (f32[8,256,256]{2,1,0:T(8,128)}, f32[8,256,256]{2,1,0:T(8,128)S(1)}, u32[]{:S(2)}, u32[]{:S(2)}) collective-permute-start(f32[8,256,256]{2,1,0:T(8,128)} %get-tuple-element.103), channel_id=1, source_target_pairs={{0,1},{1,2},{2,3},{4,5},{5,6},{6,7},{8,9},{9,10},{10,11},{12,13},{... | collective-permute-start | bytes 6291464 | tf_op jit(solution)/shard_map/ppermute | solution.py:74
  681.7 94.0 %collective-permute-start.49 = (f32[5,256,256]{2,1,0:T(8,128)}, f32[5,256,256]{2,1,0:T(8,128)S(1)}, u32[]{:S(2)}, u32[]{:S(2)}) collective-permute-start(f32[5,256,256]{2,1,0:T(8,128)} %get-tuple-element.98), channel_id=1, source_target_pairs={{3,0},{7,4},{11,8},{15,12},{19,16},{23,20},{27,24},{31,28}} | collective-permute-start | bytes 3932168 | tf_op jit(solution)/shard_map/ppermute | solution.py:79
  694.8 115.9 %collective-permute-start.58 = (f32[8,256,256]{2,1,0:T(8,128)}, f32[8,256,256]{2,1,0:T(8,128)S(1)}, u32[]{:S(2)}, u32[]{:S(2)}) collective-permute-start(f32[8,256,256]{2,1,0:T(8,128)} %get-tuple-element.106), channel_id=1, source_target_pairs={{0,1},{1,2},{2,3},{4,5},{5,6},{6,7},{8,9},{9,10},{10,11},{12,13},{... | collective-permute-start | bytes 6291464 | tf_op jit(solution)/shard_map/ppermute | solution.py:74
  708.3 102.5 %collective-permute-start.59 = (f32[7,256,256]{2,1,0:T(8,128)}, f32[7,256,256]{2,1,0:T(8,128)S(1)}, u32[]{:S(2)}, u32[]{:S(2)}) collective-permute-start(f32[7,256,256]{2,1,0:T(8,128)} %get-tuple-element.107), channel_id=1, source_target_pairs={{3,0},{7,4},{11,8},{15,12},{19,16},{23,20},{27,24},{31,28}} | collective-permute-start | bytes 5505032 | tf_op jit(solution)/shard_map/ppermute | solution.py:79
  775.7 42.7 %collective-permute-start.44 = (f32[6,256,256]{2,1,0:T(8,128)}, f32[6,256,256]{2,1,0:T(8,128)S(1)}, u32[]{:S(2)}, u32[]{:S(2)}) collective-permute-start(f32[6,256,256]{2,1,0:T(8,128)} %get-tuple-element.94), channel_id=1, source_target_pairs={{0,1},{1,2},{2,3},{4,5},{5,6},{6,7},{8,9},{9,10},{10,11},{12,13},{... | collective-permute-start | bytes 4718600 | tf_op jit(solution)/shard_map/ppermute | solution.py:74
  777.1 71.6 %collective-permute-start.48 = (f32[6,256,256]{2,1,0:T(8,128)}, f32[6,256,256]{2,1,0:T(8,128)S(1)}, u32[]{:S(2)}, u32[]{:S(2)}) collective-permute-start(f32[6,256,256]{2,1,0:T(8,128)} %get-tuple-element.97), channel_id=1, source_target_pairs={{0,1},{1,2},{2,3},{4,5},{5,6},{6,7},{8,9},{9,10},{10,11},{12,13},{... | collective-permute-start | bytes 4718600 | tf_op jit(solution)/shard_map/ppermute | solution.py:74
  778.5 71.6 %collective-permute-start.51 = (f32[6,256,256]{2,1,0:T(8,128)}, f32[6,256,256]{2,1,0:T(8,128)}, u32[]{:S(2)}, u32[]{:S(2)}) collective-permute-start(f32[6,256,256]{2,1,0:T(8,128)} %get-tuple-element.99.rt), channel_id=1, source_target_pairs={{0,28},{4,0},{8,4},{12,8},{16,12},{20,16},{24,20},{28,24},{1,29},{... | collective-permute-start | bytes 4718600 | tf_op jit(solution)/shard_map/ppermute | solution.py:68
  810.7 80.7 %collective-permute-start.57 = (f32[8,256,256]{2,1,0:T(8,128)}, f32[8,256,256]{2,1,0:T(8,128)S(1)}, u32[]{:S(2)}, u32[]{:S(2)}) collective-permute-start(f32[8,256,256]{2,1,0:T(8,128)} %get-tuple-element.105.rb), channel_id=1, source_target_pairs={{0,4},{4,8},{8,12},{12,16},{16,20},{20,24},{24,28},{28,0},{1,5},{5... | collective-permute-start | bytes 6291464 | tf_op jit(solution)/shard_map/ppermute | solution.py:68
  810.7 80.8 %collective-permute-start.61 = (f32[8,256,256]{2,1,0:T(8,128)}, f32[8,256,256]{2,1,0:T(8,128)}, u32[]{:S(2)}, u32[]{:S(2)}) collective-permute-start(f32[8,256,256]{2,1,0:T(8,128)} %get-tuple-element.108.rt), channel_id=1, source_target_pairs={{0,28},{4,0},{8,4},{12,8},{16,12},{20,16},{24,20},{28,24},{1,29},{... | collective-permute-start | bytes 6291464 | tf_op jit(solution)/shard_map/ppermute | solution.py:68
  818.4 103.2 %collective-permute-start.56 = (f32[8,256,256]{2,1,0:T(8,128)}, f32[8,256,256]{2,1,0:T(8,128)}, u32[]{:S(2)}, u32[]{:S(2)}) collective-permute-start(f32[8,256,256]{2,1,0:T(8,128)} %pad_add_fusion.1.lb), channel_id=1, source_target_pairs={{0,4},{4,8},{8,12},{12,16},{16,20},{20,24},{24,28},{28,0},{1,5},{5... | collective-permute-start | bytes 6291464 | tf_op jit(solution)/shard_map/ppermute | solution.py:68
  848.6 75.7 %collective-permute-start.60 = (f32[8,256,256]{2,1,0:T(8,128)}, f32[8,256,256]{2,1,0:T(8,128)}, u32[]{:S(2)}, u32[]{:S(2)}) collective-permute-start(f32[8,256,256]{2,1,0:T(8,128)} %pad_add_fusion.lt), channel_id=1, source_target_pairs={{0,28},{4,0},{8,4},{12,8},{16,12},{20,16},{24,20},{28,24},{1,29},{... | collective-permute-start | bytes 6291464 | tf_op jit(solution)/shard_map/ppermute | solution.py:68
  850.0 71.5 %collective-permute-start.50 = (f32[6,256,256]{2,1,0:T(8,128)}, f32[6,256,256]{2,1,0:T(8,128)}, u32[]{:S(2)}, u32[]{:S(2)}) collective-permute-start(f32[6,256,256]{2,1,0:T(8,128)} %pad_add_fusion.2.lt), channel_id=1, source_target_pairs={{0,28},{4,0},{8,4},{12,8},{16,12},{20,16},{24,20},{28,24},{1,29},{... | collective-permute-start | bytes 4718600 | tf_op jit(solution)/shard_map/ppermute | solution.py:68
  891.5 116.8 %collective-permute-start.29 = (f32[2,256,256]{2,1,0:T(8,128)}, f32[2,256,256]{2,1,0:T(8,128)}, u32[]{:S(2)}, u32[]{:S(2)}) collective-permute-start(f32[2,256,256]{2,1,0:T(8,128)} %get-tuple-element.80.rt), channel_id=1, source_target_pairs={{0,28},{4,0},{8,4},{12,8},{16,12},{20,16},{24,20},{28,24},{1,29},{... | collective-permute-start | bytes 1572872 | tf_op jit(solution)/shard_map/ppermute | solution.py:68
  891.5 62.9 %collective-permute-start.41 = (f32[4,256,256]{2,1,0:T(8,128)}, f32[4,256,256]{2,1,0:T(8,128)S(1)}, u32[]{:S(2)}, u32[]{:S(2)}) collective-permute-start(f32[4,256,256]{2,1,0:T(8,128)} %get-tuple-element.90.rt), channel_id=1, source_target_pairs={{0,28},{4,0},{8,4},{12,8},{16,12},{20,16},{24,20},{28,24},{1,29},{... | collective-permute-start | bytes 3145736 | tf_op jit(solution)/shard_map/ppermute | solution.py:68
  921.5 38.1 %collective-permute-start.47 = (f32[6,256,256]{2,1,0:T(8,128)}, f32[6,256,256]{2,1,0:T(8,128)}, u32[]{:S(2)}, u32[]{:S(2)}) collective-permute-start(f32[6,256,256]{2,1,0:T(8,128)} %get-tuple-element.96.rb), channel_id=1, source_target_pairs={{0,4},{4,8},{8,12},{12,16},{16,20},{20,24},{24,28},{28,0},{1,5},{5... | collective-permute-start | bytes 4718600 | tf_op jit(solution)/shard_map/ppermute | solution.py:68
  921.6 55.3 %collective-permute-start.40 = (f32[4,256,256]{2,1,0:T(8,128)}, f32[4,256,256]{2,1,0:T(8,128)}, u32[]{:S(2)}, u32[]{:S(2)}) collective-permute-start(f32[4,256,256]{2,1,0:T(8,128)} %pad_add_fusion.4.lt), channel_id=1, source_target_pairs={{0,28},{4,0},{8,4},{12,8},{16,12},{20,16},{24,20},{28,24},{1,29},{... | collective-permute-start | bytes 3145736 | tf_op jit(solution)/shard_map/ppermute | solution.py:68
  924.3 64.8 %collective-permute-start.46 = (f32[6,256,256]{2,1,0:T(8,128)}, f32[6,256,256]{2,1,0:T(8,128)}, u32[]{:S(2)}, u32[]{:S(2)}) collective-permute-start(f32[6,256,256]{2,1,0:T(8,128)} %pad_add_fusion.3.lb), channel_id=1, source_target_pairs={{0,4},{4,8},{8,12},{12,16},{16,20},{20,24},{24,28},{28,0},{1,5},{5... | collective-permute-start | bytes 4718600 | tf_op jit(solution)/shard_map/ppermute | solution.py:68
  954.4 78.9 %collective-permute-start.31 = (f32[2,256,256]{2,1,0:T(8,128)}, f32[2,256,256]{2,1,0:T(8,128)}, u32[]{:S(2)}, u32[]{:S(2)}) collective-permute-start(f32[2,256,256]{2,1,0:T(8,128)} %get-tuple-element.81.rb), channel_id=1, source_target_pairs={{0,4},{4,8},{8,12},{12,16},{16,20},{20,24},{24,28},{28,0},{1,5},{5... | collective-permute-start | bytes 1572872 | tf_op jit(solution)/shard_map/ppermute | solution.py:68
  959.6 50.3 %collective-permute-start.37 = (f32[4,256,256]{2,1,0:T(8,128)}, f32[4,256,256]{2,1,0:T(8,128)S(1)}, u32[]{:S(2)}, u32[]{:S(2)}) collective-permute-start(f32[4,256,256]{2,1,0:T(8,128)} %get-tuple-element.87.rb), channel_id=1, source_target_pairs={{0,4},{4,8},{8,12},{12,16},{16,20},{20,24},{24,28},{28,0},{1,5},{5... | collective-permute-start | bytes 3145736 | tf_op jit(solution)/shard_map/ppermute | solution.py:68
  (39 other events, 711.6 us)
Sparse Core Ops, SparseCore 0:
  9.1 83.4 all-gather.4
  94.2 148.0 all-gather.2
